TPU v7x, 32 devices: a whole 2x2x4 slice. The times are simulated.
32 devices in a mesh: dp: 4 (over x, core), wide: 8 (over z, y).
Axes of the slice: x: 2, y: 2, z: 4, core: 2. Of those that a mesh axis runs over, the one named last changes fastest.
Arguments:
- real_images: bfloat16 [384, 8, 8, 640], P(('dp', 'wide')), may hold values from -6 to 6
- replay_chains: bfloat16 [384, 8, 8, 640], P(('dp', 'wide')), may hold values from -1 to 1
- langevin_noise: bfloat16 [2, 384, 8, 8, 640], P(None, ('dp', 'wide')), may hold values from -16 to 16
- real_cot: bfloat16 [384, 8, 8, 640], P(('dp', 'wide')), may hold values from -6 to 6
- chain_cot: bfloat16 [384, 8, 8, 640], P(('dp', 'wide')), may hold values from -6 to 6
- kernel_one: bfloat16 [3, 3, 640, 640], P(None, None, 'wide'), may hold values from -0.125 to 0.125
- bias_one: bfloat16 [640], P('wide'), may hold values from -3 to 3
- kernel_two: bfloat16 [3, 3, 640, 640], P(None, None, 'wide'), may hold values from -0.125 to 0.125
- bias_two: bfloat16 [640], P('wide'), may hold values from -3 to 3
Outputs:
- block_output: float32 [384, 8, 8, 640], P(('dp', 'wide'))
- input_grad: float32 [384, 8, 8, 640], P(('dp', 'wide'))
- final_samples: float32 [384, 8, 8, 640], P(('dp', 'wide'))
- kernel_one_grad: float32 [3, 3, 640, 640], P(None, None, 'wide')
- bias_one_grad: float32 [640], P('wide')
- kernel_two_grad: float32 [3, 3, 640, 640], P(None, None, 'wide')
- bias_two_grad: float32 [640], P('wide')
All inputs are finite; a program needn't handle non-finite values.
Results may differ from a plain program's by a relative error of at most 0.015.
The roundings to bfloat16 on the way count: a program that leaves them out, or rounds other values in their place, can miss the bound.
Values may be sent and summed in bfloat16 or wider, within the bound.
A program may use at most 256 MiB of HBM per device.

v0:
```python
import jax
import jax.numpy as jnp
from jax import lax
from jax.sharding import PartitionSpec as P


def leaky_relu(values):
    return jnp.where(values > 0, values, 0.2 * values)


def leak_slope(values):
    return jnp.where(values > 0, 1.0, 0.2).astype(jnp.float32)


def tap_patches(activation):
    batch_size, height, map_width, channels = activation.shape
    padded = jnp.pad(activation, ((0, 0), (1, 1), (1, 1), (0, 0)))
    tap_list = [
        padded[:, row_off : row_off + height, col_off : col_off + map_width, :]
        for row_off in range(3)
        for col_off in range(3)
    ]
    return jnp.stack(tap_list, axis=3).reshape(batch_size * height * map_width, 9 * channels)


def conv_apply(activation, kernel_mat, bias_row):
    result = jnp.dot(tap_patches(activation), kernel_mat, preferred_element_type=jnp.float32)
    return result.reshape(activation.shape[:3] + (kernel_mat.shape[1],)) + bias_row.astype(
        jnp.float32
    )


def conv_back(gradient, kernel_mat):
    batch_size, height, map_width, channels = gradient.shape
    in_channels = kernel_mat.shape[0] // 9
    spread = lax.dot_general(
        gradient.reshape(-1, channels),
        kernel_mat,
        (((1,), (1,)), ((), ())),
        preferred_element_type=jnp.float32,
    )
    spread = spread.reshape(batch_size, height, map_width, 9, in_channels)
    summed = jnp.zeros((batch_size, height + 2, map_width + 2, in_channels), jnp.float32)
    for row_off in range(3):
        for col_off in range(3):
            summed = summed + jnp.pad(
                spread[:, :, :, 3 * row_off + col_off, :],
                ((0, 0), (row_off, 2 - row_off), (col_off, 2 - col_off), (0, 0)),
            )
    return summed[:, 1 : height + 1, 1 : map_width + 1, :]


def kernel_partial(activation, gradient):
    channels = gradient.shape[3]
    return lax.dot_general(
        tap_patches(activation),
        gradient.reshape(-1, channels),
        (((0,), (0,)), ((), ())),
        preferred_element_type=jnp.float32,
    )


def hidden_pass(inputs_now, kernel_mats):
    lower_act = leaky_relu(inputs_now).astype(jnp.bfloat16)
    hidden = conv_apply(lower_act, kernel_mats[0], kernel_mats[1])
    return (lower_act, hidden)


def hidden_gradient(hidden, cotangent, kernel_mats):
    inner_grad = conv_back(cotangent, kernel_mats[2])
    return (inner_grad * leak_slope(hidden)).astype(jnp.bfloat16)


def input_gradient(inputs_now, cotangent, hidden_grad, kernel_mats):
    return cotangent.astype(jnp.float32) + leak_slope(inputs_now) * conv_back(
        hidden_grad, kernel_mats[0]
    )


def param_partials(lower_act, hidden_grad, upper_act, cotangent):
    return (
        kernel_partial(lower_act, hidden_grad),
        jnp.sum(hidden_grad.astype(jnp.float32), axis=(0, 1, 2)),
        kernel_partial(upper_act, cotangent),
        jnp.sum(cotangent.astype(jnp.float32), axis=(0, 1, 2)),
    )


def local(
    real_images,
    replay_chains,
    langevin_noise,
    real_cot,
    chain_cot,
    kernel_one,
    bias_one,
    kernel_two,
    bias_two,
):

    def as_mats(gathered):
        rows_all = 9 * gathered[0].shape[2]
        return (
            gathered[0].reshape(rows_all, gathered[0].shape[3]),
            gathered[1],
            gathered[2].reshape(rows_all, gathered[2].shape[3]),
            gathered[3],
        )

    def fetch_kernels():
        return as_mats(
            (
                lax.all_gather(kernel_one, "wide", axis=2, tiled=True),
                lax.all_gather(bias_one, "wide", axis=0, tiled=True),
                lax.all_gather(kernel_two, "wide", axis=2, tiled=True),
                lax.all_gather(bias_two, "wide", axis=0, tiled=True),
            )
        )

    chain_state = replay_chains.astype(jnp.float32)
    for step_index in range(langevin_noise.shape[0]):
        kernel_mats = fetch_kernels()
        lower_act, hidden = hidden_pass(chain_state, kernel_mats)
        kernel_mats = fetch_kernels()
        hidden_grad = hidden_gradient(hidden, chain_cot, kernel_mats)
        pull_grad = input_gradient(chain_state, chain_cot, hidden_grad, kernel_mats)
        chain_state = (
            chain_state - pull_grad + 0.01 * langevin_noise[step_index].astype(jnp.float32)
        )
    real_input = real_images.astype(jnp.float32)
    kernel_mats = fetch_kernels()
    real_lower, real_hidden = hidden_pass(real_input, kernel_mats)
    real_upper = leaky_relu(real_hidden).astype(jnp.bfloat16)
    block_output = real_input + conv_apply(real_upper, kernel_mats[2], kernel_mats[3])
    sample_lower, sample_hidden = hidden_pass(chain_state, kernel_mats)
    sample_upper = leaky_relu(sample_hidden).astype(jnp.bfloat16)
    kernel_mats = fetch_kernels()
    real_hgrad = hidden_gradient(real_hidden, real_cot, kernel_mats)
    input_grad = input_gradient(real_input, real_cot, real_hgrad, kernel_mats)
    real_terms = param_partials(real_lower, real_hgrad, real_upper, real_cot)
    negated_cot = -chain_cot
    sample_hgrad = hidden_gradient(sample_hidden, negated_cot, kernel_mats)
    sample_terms = param_partials(sample_lower, sample_hgrad, sample_upper, negated_cot)
    totals = tuple(
        (real_term + sample_term for real_term, sample_term in zip(real_terms, sample_terms))
    )
    channels = kernel_one.shape[3]
    kernel_shape = (3, 3, channels, channels)
    shares = (
        lax.psum_scatter(totals[0].reshape(kernel_shape), "wide", scatter_dimension=2, tiled=True),
        lax.psum_scatter(totals[1], "wide", scatter_dimension=0, tiled=True),
        lax.psum_scatter(totals[2].reshape(kernel_shape), "wide", scatter_dimension=2, tiled=True),
        lax.psum_scatter(totals[3], "wide", scatter_dimension=0, tiled=True),
    )
    summed = lax.psum((shares[0], shares[1], shares[2], shares[3]), "dp")
    return (block_output, input_grad, chain_state, summed[0], summed[1], summed[2], summed[3])


def solution(mesh):
    return jax.shard_map(
        local,
        mesh=mesh,
        in_specs=(
            P(("dp", "wide"), None, None, None),
            P(("dp", "wide"), None, None, None),
            P(None, ("dp", "wide"), None, None, None),
            P(("dp", "wide"), None, None, None),
            P(("dp", "wide"), None, None, None),
            P(None, None, "wide", None),
            P("wide"),
            P(None, None, "wide", None),
            P("wide"),
        ),
        out_specs=(
            P(("dp", "wide"), None, None, None),
            P(("dp", "wide"), None, None, None),
            P(("dp", "wide"), None, None, None),
            P(None, None, "wide", None),
            P("wide"),
            P(None, None, "wide", None),
            P("wide"),
        ),
        check_vma=False,
    )
```

profile of v0, /device:TPU:0, one launch (start us, length us, event | category | flops | bytes accessed | tf_op | source)
XLA Modules:
  0.0 1033.8 jit_solution(8459444132894927634)
XLA Ops:
  8.7 1.3 fusion.141
  12.4 24.1 %all-reduce.67 = (bf16[640]{0:T(1024)(128)(2,1)S(1)}, bf16[640]{0:T(1024)(128)(2,1)}) all-reduce(bf16[640]{0:T(1024)(128)(2,1)S(1)} %dynamic-update-slice, bf16[640]{0:T(1024)(128)(2,1)S(1)} %dynamic-update-slice.1), channel_id=1, replica_groups=mesh['dp'=4,'wide'=8] {'wide'}, use_global_device_ids=true, to_apply=%add.60 | all-reduce | flops 1280 | bytes 5120
  40.2 1.2 fusion.31
  41.4 1.2 bitcast_dynamic-update-slice_fusion.5
  46.2 1.2 fusion.39
  47.4 7.8 copy.134
  59.0 1.2 fusion.63
  60.2 1.2 bitcast_dynamic-update-slice_fusion.3
  65.0 1.2 fusion.71
  66.2 7.9 copy.163
  74.1 51.5 %all-gather.5.cloned.1.call-done = bf16[3,3,640,640]{3,2,1,0:T(8,128)(2,1)} async-done(((bf16[3,3,80,640]{3,2,1,0:T(8,128)(2,1)}), bf16[3,3,640,640]{3,2,1,0:T(8,128)(2,1)}) %all-gather.5.cloned.1.call-update) | async-done | bytes 7372816 | tf_op jit(solution)/shard_map/all_gather | solution.py:115
  125.5 13.1 %fusion.122 = f32[12,8,8,9,640]{4,2,1,0,3:T(8,128)} fusion(bf16[9,640,640,1,1]{2,1,4,3,0:T(8,128)(2,1)} %bitcast.423, bf16[12,8,8,640]{3,2,1,0:T(8,128)(2,1)S(1)} %copy-done.2), kind=kOutput, calls=%fused_computation.301 | convolution fusion | flops 5662310400 | bytes 26050560 | tf_op jit(solution)/shard_map/dot_general | solution.py:36
  138.7 13.4 %slice_bitcast_fusion.35 = (f32[12,8,8,640]{3,2,1,0:T(8,128)}, f32[12,8,8,640]{3,2,1,0:T(8,128)}, f32[12,8,8,640]{3,2,1,0:T(8,128)}, f32[12,8,8,640]{3,2,1,0:T(8...) fusion(f32[12,8,8,9,640]{4,2,1,0,3:T(8,128)} %fusion.122), kind=kLoop, calls=%fused_computation.157 | loop fusion | bytes 35389440 | tf_op jit(solution)/shard_map/squeeze | solution.py:47
  152.4 10.0 fusion.120
  162.5 75.9 %all-gather.3.cloned.1.call-done = bf16[3,3,640,640]{3,2,1,0:T(8,128)(2,1)} async-done(((bf16[3,3,80,640]{3,2,1,0:T(8,128)(2,1)}), bf16[3,3,640,640]{3,2,1,0:T(8,128)(2,1)}) %all-gather.3.cloned.1.call-update) | async-done | bytes 7372816 | tf_op jit(solution)/shard_map/all_gather | solution.py:113
  238.4 13.0 %fusion.142 = f32[12,8,8,640]{3,2,1,0:T(8,128)} fusion(bf16[12,8,8,5760]{3,2,1,0:T(8,128)(2,1)} %bitcast.412, bf16[5760,640,1,1]{1,0,3,2:T(8,128)(2,1)} %bitcast.399), kind=kOutput, calls=%fused_computation.319 | convolution fusion | flops 5662310400 | bytes 18186240 | tf_op jit(solution)/shard_map/dot_general | solution.py:27
  256.3 27.9 %fusion.129 = f32[12,8,8,9,640]{4,2,1,0,3:T(8,128)} fusion(bf16[9,640,640,1,1]{2,1,4,3,0:T(8,128)(2,1)} %bitcast.401, f32[12,8,8,640]{3,2,1,0:T(8,128)S(1)} %pad_add_fusion.24, bf16[12,8,8,5760]{3,2,1,0:T(8,128)(2,1)} %bitcast.408, bf16[5760,640,1,1]{1,0,3,2:T(8,128)(2,1)} %bitcast.400, f32[640]{0:T(1024)S(1)} %convert_element_type.154), kind=kOutput, calls=%fused_computation.310 | convolution fusion | flops 11327078400 | bytes 43256320 | tf_op jit(solution)/shard_map/dot_general | solution.py:36
  284.1 8.2 slice_bitcast_fusion.26
  292.4 2.5 pad_add_fusion.2
  295.0 3.0 fusion.8
  308.4 7.8 copy.173
  316.1 27.9 %fusion.128 = f32[12,8,8,9,640]{4,2,1,0,3:T(8,128)} fusion(bf16[9,640,640,1,1]{2,1,4,3,0:T(8,128)(2,1)} %bitcast.403, f32[12,8,8,640]{3,2,1,0:T(8,128)S(1)} %pad_add_fusion.24, bf16[12,8,8,5760]{3,2,1,0:T(8,128)(2,1)} %bitcast.409, bf16[5760,640,1,1]{1,0,3,2:T(8,128)(2,1)} %bitcast.402, f32[640]{0:T(1024)S(1)} %convert_element_type.154), kind=kOutput, calls=%fused_computation.309 | convolution fusion | flops 11327078400 | bytes 43256320 | tf_op jit(solution)/shard_map/dot_general | solution.py:36
  344.0 6.8 slice_bitcast_fusion.17
  353.2 4.1 fusion.13
  367.7 7.8 copy.184
  375.5 11.6 %slice_bitcast_fusion.8 = (f32[12,8,8,640]{3,2,1,0:T(8,128)S(1)}, f32[12,8,8,640]{3,2,1,0:T(8,128)S(1)}, f32[12,8,8,640]{3,2,1,0:T(8,128)}, f32[12,8,8,640]{3,2,...) fusion(f32[12,8,8,9,640]{4,2,1,0,3:T(8,128)} %fusion.120), kind=kLoop, calls=%fused_computation.112 | loop fusion | bytes 35389440 | tf_op jit(solution)/shard_map/squeeze | solution.py:47
  387.1 14.1 %fusion.126 = f32[12,8,8,9,640]{4,2,1,0,3:T(8,128)} fusion(bf16[9,640,640,1,1]{2,1,4,3,0:T(8,128)(2,1)} %bitcast.424, bf16[12,8,8,640]{3,2,1,0:T(8,128)(2,1)} %param.12), kind=kOutput, calls=%fused_computation.305 | convolution fusion | flops 5662310400 | bytes 26050560 | tf_op jit(solution)/shard_map/dot_general | solution.py:36
  401.2 11.4 %slice_bitcast_fusion.53 = (f32[12,8,8,640]{3,2,1,0:T(8,128)S(1)}, f32[12,8,8,640]{3,2,1,0:T(8,128)}, f32[12,8,8,640]{3,2,1,0:T(8,128)}, f32[12,8,8,640]{3,2,1,0...) fusion(f32[12,8,8,9,640]{4,2,1,0,3:T(8,128)} %fusion.126), kind=kLoop, calls=%fused_computation.187 | loop fusion | bytes 35389440 | tf_op jit(solution)/shard_map/squeeze | solution.py:47
  412.7 11.1 %fusion.23 = (u16[8,8,640]{2,1,0:T(8,128)(2,1)S(1)}, u16[8,8,640]{2,1,0:T(8,128)(2,1)S(1)}, f32[12,8,8,640]{3,2,1,0:T(8,128)}) fusion(f32[640]{0:T(1024)S(1)} %convert_element_type.154, f32[12,8,8,640]{3,2,1,0:T(8,128)S(1)} %copy-done.22, bf16[12,8,8,5760]{3,2,1,0:T(8,128)(2,1)} %bitcast.416, bf16[5760,640,1,1]{1,0,3,2:T(8,128)(2,1)S(1)} %bitcast.407), kind=kOutput, calls=%fused_computation.198 | convolution fusion | flops 5668126720 | bytes 20318720 | tf_op jit(solution)/shard_map/dot_general | solution.py:27
  426.3 11.4 %convert_reduce_fusion.2 = (f32[640]{0:T(1024)S(1)}, bf16[12,8,8,640]{3,2,1,0:T(8,128)(2,1)}, bf16[12,8,8,640]{3,2,1,0:T(8,128)(2,1)S(1)}, bf16[12,8,8,640]{3,2,...) fusion(u16[8,8,640]{2,1,0:T(8,128)(2,1)S(1)} %get-tuple-element.7, ...), kind=kLoop, calls=%fused_computation.189 | loop fusion | flops 18184960 | bytes 35560960 | tf_op jit(solution)/shard_map/reduce_sum | solution.py:83
  437.7 13.1 %fusion.143 = f32[5760,640]{1,0:T(8,128)} fusion(bf16[768,5760]{1,0:T(8,128)(2,1)} %bitcast.413, bf16[768,640]{1,0:T(8,128)(2,1)} %bitcast.420), kind=kOutput, calls=%fused_computation.320 | convolution fusion | flops 5662310400 | bytes 24576000 | tf_op jit(solution)/shard_map/dot_general | solution.py:55
  450.8 15.0 %convolution_add_fusion.1 = f32[5760,640]{1,0:T(8,128)} fusion(f32[5760,640]{1,0:T(8,128)} %fusion.143, bf16[768,5760]{1,0:T(8,128)(2,1)} %bitcast.417, bf16[768,640]{1,0:T(8,128)(2,1)S(1)} %bitcast.422), kind=kOutput, calls=%fused_computation.1 | convolution fusion | flops 5665996800 | bytes 39321600 | tf_op jit(solution)/shard_map/dot_general | solution.py:55
  477.5 7.6 copy.135
  495.5 7.9 copy.196
  503.4 13.2 %fusion.144 = f32[5760,640]{1,0:T(8,128)} fusion(bf16[768,5760]{1,0:T(8,128)(2,1)} %bitcast.414, bf16[768,640]{1,0:T(8,128)(2,1)S(1)} %bitcast.419), kind=kOutput, calls=%fused_computation.321 | convolution fusion | flops 5662310400 | bytes 24576000 | tf_op jit(solution)/shard_map/dot_general | solution.py:55
  516.6 15.7 %convolution_add_fusion = f32[5760,640]{1,0:T(8,128)} fusion(f32[5760,640]{1,0:T(8,128)} %fusion.144, bf16[768,5760]{1,0:T(8,128)(2,1)S(1)} %bitcast.418, bf16[768,640]{1,0:T(8,128)(2,1)S(1)} %bitcast.421), kind=kOutput, calls=%fused_computation | convolution fusion | flops 5665996800 | bytes 39321600 | tf_op jit(solution)/shard_map/dot_general | solution.py:55
  533.6 13.5 %fusion.124 = f32[12,8,8,9,640]{4,2,1,0,3:T(8,128)} fusion(bf16[9,640,640,1,1]{2,1,4,3,0:T(8,128)(2,1)} %bitcast.404, bf16[12,8,8,640]{3,2,1,0:T(8,128)(2,1)S(1)} %copy-done.26), kind=kOutput, calls=%fused_computation.303 | convolution fusion | flops 5662310400 | bytes 26050560 | tf_op jit(solution)/shard_map/dot_general | solution.py:36
  547.1 9.3 slice_bitcast_fusion.44
  556.4 3.1 pad_add_fusion.4
  559.6 4.5 convert_reduce_fusion
  564.1 20.0 %all-reduce.64 = (f32[640]{0:T(1024)S(1)}, f32[640]{0:T(1024)S(1)}) all-reduce(f32[640]{0:T(1024)S(1)} %add.414, f32[640]{0:T(1024)S(1)} %add.416), channel_id=3, replica_groups=mesh['dp'=4,'wide'=8] {'wide'}, use_global_device_ids=true, to_apply=%region_4.5.clone | all-reduce | flops 1280 | bytes 10240
  584.2 6.5 all-reduce.65
  590.8 111.7 %reduce-scatter.3.cloned.1.call-done = f32[3,3,80,640]{3,2,1,0:T(8,128)} async-done(((f32[3,3,640,640]{3,2,1,0:T(8,128)}), f32[3,3,80,640]{3,2,1,0:T(8,128)}) %reduce-scatter.3.cloned.1.call-update) | async-done | bytes 1843216 | tf_op jit(solution)/shard_map/reduce_scatter | solution.py:150
  702.5 241.0 %reduce-scatter.5.cloned.1.call-done = f32[3,3,80,640]{3,2,1,0:T(8,128)} async-done(((f32[3,3,640,640]{3,2,1,0:T(8,128)}), f32[3,3,80,640]{3,2,1,0:T(8,128)}) %reduce-scatter.5.cloned.1.call-update) | async-done | bytes 1843216 | tf_op jit(solution)/shard_map/reduce_scatter | solution.py:152
  943.5 12.7 %convert_add_fusion = f32[12,8,8,640]{3,2,1,0:T(8,128)} fusion(bf16[12,8,8,640]{3,2,1,0:T(8,128)(2,1)S(1)} %copy-done.6, bf16[12,8,8,5760]{3,2,1,0:T(8,128)(2,1)} %bitcast.415, bf16[5760,640,1,1]{1,0,3,2:T(8,128)(2,1)} %bitcast.425, f32[640]{0:T(1024)S(1)} %convert_element_type.156), kind=kOutput, calls=%fused_computation.61 | convolution fusion | flops 5663784960 | bytes 19171840 | tf_op jit(solution)/shard_map/dot_general | solution.py:27
  956.2 66.4 %all-reduce.70.cloned.1.call-done = (f32[3,3,80,640]{3,2,1,0:T(8,128)}, f32[3,3,80,640]{3,2,1,0:T(8,128)}) async-done(((f32[3,3,80,640]{3,2,1,0:T(8,128)}, f32[3,3,80,640]{3,2,1,0:T(8,128)}), (f32[3,3,80,640]{3,2,1,0:T(8,128)}, f32[3,3,80,640]{3,2,1,0:T(8,128)})) %all-reduce.70.cloned.1.call-update) | async-done | bytes 3686416 | tf_op jit(solution)/shard_map/psum | solution.py:155
  1022.6 3.0 copy.259
  1025.6 1.2 copy.260
  (145 shorter events, 71.3 us)
Async XLA Ops:
  7.2 29.3 %copy-start.5 = (bf16[12,8,8,640]{3,2,1,0:T(8,128)(2,1)S(1)}, bf16[12,8,8,640]{3,2,1,0:T(8,128)(2,1)}, u32[]{:S(2)}) copy-start(bf16[12,8,8,640]{3,2,1,0:T(8,128)(2,1)} %param.9) | copy-start | bytes 2949124
  7.2 118.4 %all-gather.5.cloned.1.call-start = ((), (), s32[]{:S(2)}) async-start(), calls=%async_computation.3 | async-start | bytes 8294400 | tf_op jit(solution)/shard_map/all_gather | solution.py:115
  7.9 230.5 %all-gather.3.cloned.1.call-start = ((), (), s32[]{:S(2)}) async-start(), calls=%async_computation.2 | async-start | bytes 8294400 | tf_op jit(solution)/shard_map/all_gather | solution.py:113
  8.7 693.8 %reduce-scatter.3.cloned.1.call-start = ((), (), s32[]{:S(2)}) async-start(), calls=%async_computation.4 | async-start | bytes 16588800 | tf_op jit(solution)/shard_map/reduce_scatter | solution.py:150
  47.4 7.8 copy-start.1
  66.2 59.3 %copy-start.2 = (bf16[12,8,8,640]{3,2,1,0:T(8,128)(2,1)S(1)}, bf16[12,8,8,640]{3,2,1,0:T(8,128)(2,1)}, u32[]{:S(2)}) copy-start(bf16[12,8,8,640]{3,2,1,0:T(8,128)(2,1)} %param.13) | copy-start | bytes 2949124
  138.7 13.8 %copy-start.31 = (bf16[3,3,640,640]{3,2,1,0:T(8,128)(2,1)S(1)}, bf16[3,3,640,640]{3,2,1,0:T(8,128)(2,1)}, u32[]{:S(2)}) copy-start(bf16[3,3,640,640]{3,2,1,0:T(8,128)(2,1)} %all-gather.5.cloned.1.call-done) | copy-start | bytes 22118404
  238.4 13.0 %copy-start.16 = (f32[12,8,8,640]{3,2,1,0:T(8,128)S(1)}, f32[12,8,8,640]{3,2,1,0:T(8,128)}, u32[]{:S(2)}) copy-start(f32[12,8,8,640]{3,2,1,0:T(8,128)} %get-tuple-element.70) | copy-start | bytes 5898244
  238.4 13.0 %copy-start.17 = (f32[12,8,8,640]{3,2,1,0:T(8,128)S(1)}, f32[12,8,8,640]{3,2,1,0:T(8,128)}, u32[]{:S(2)}) copy-start(f32[12,8,8,640]{3,2,1,0:T(8,128)} %get-tuple-element.76) | copy-start | bytes 5898244
  238.4 13.0 %copy-start.18 = (f32[12,8,8,640]{3,2,1,0:T(8,128)S(1)}, f32[12,8,8,640]{3,2,1,0:T(8,128)}, u32[]{:S(2)}) copy-start(f32[12,8,8,640]{3,2,1,0:T(8,128)} %get-tuple-element.77) | copy-start | bytes 5898244
  238.4 13.9 %copy-start.15 = (f32[12,8,8,640]{3,2,1,0:T(8,128)S(1)}, f32[12,8,8,640]{3,2,1,0:T(8,128)}, u32[]{:S(2)}) copy-start(f32[12,8,8,640]{3,2,1,0:T(8,128)} %get-tuple-element.78) | copy-start | bytes 5898244
  251.4 1.5 copy-start.10
  251.4 2.1 copy-start.11
  251.4 2.7 copy-start.12
  251.5 3.3 copy-start.13
  251.5 3.8 copy-start.14
  292.4 2.5 copy-start.3
  292.4 2.5 copy-start.20
  350.8 1.2 copy-start.4
  350.8 1.8 copy-start.19
  350.8 2.4 copy-start.21
  375.5 37.2 %slice-start = ((s8[7372800]{0:T(1024)(128)(4,1)}), s8[4194304]{0:T(1024)(128)(4,1)S(1)}, s32[]{:S(2)}) async-start(s8[7372800]{0:T(1024)(128)(4,1)} %bitcast.405), calls=%async_computation.7 | async-start | bytes 8388608
  387.0 25.6 %slice-start.1 = ((s8[7372800]{0:T(1024)(128)(4,1)}), s8[3178496]{0:T(1024)(128)(4,1)S(1)}, s32[]{:S(2)}) async-start(s8[7372800]{0:T(1024)(128)(4,1)} %bitcast.405), calls=%async_computation.8 | async-start | bytes 6356992
  401.2 11.5 %copy-start.22 = (f32[12,8,8,640]{3,2,1,0:T(8,128)S(1)}, f32[12,8,8,640]{3,2,1,0:T(8,128)}, u32[]{:S(2)}) copy-start(f32[12,8,8,640]{3,2,1,0:T(8,128)} %fusion.142) | copy-start | bytes 5898244
  412.7 11.2 %copy-start.7 = (f32[12,8,8,640]{3,2,1,0:T(8,128)S(1)}, f32[12,8,8,640]{3,2,1,0:T(8,128)}, u32[]{:S(2)}) copy-start(f32[12,8,8,640]{3,2,1,0:T(8,128)} %get-tuple-element.31) | copy-start | bytes 5898244
  412.7 11.2 %copy-start.8 = (f32[12,8,8,640]{3,2,1,0:T(8,128)S(1)}, f32[12,8,8,640]{3,2,1,0:T(8,128)}, u32[]{:S(2)}) copy-start(f32[12,8,8,640]{3,2,1,0:T(8,128)} %get-tuple-element.32) | copy-start | bytes 5898244
  423.9 1.5 copy-start.9
  437.7 13.1 %copy-start.28 = (bf16[12,8,8,640]{3,2,1,0:T(8,128)(2,1)S(1)}, bf16[12,8,8,640]{3,2,1,0:T(8,128)(2,1)}, u32[]{:S(2)}) copy-start(bf16[12,8,8,640]{3,2,1,0:T(8,128)(2,1)} %get-tuple-element.18) | copy-start | bytes 2949124
  465.8 477.7 %reduce-scatter.5.cloned.1.call-start = ((), (), s32[]{:S(2)}) async-start(), calls=%async_computation.5 | async-start | bytes 16588800 | tf_op jit(solution)/shard_map/reduce_scatter | solution.py:152
  495.5 7.9 copy-start.24
  503.4 13.2 %copy-start = (bf16[12,8,8,9,640]{4,2,3,1,0:T(8,128)(2,1)S(1)}, bf16[12,8,8,9,640]{4,2,3,1,0:T(8,128)(2,1)}, u32[]{:S(2)}) copy-start(bf16[12,8,8,9,640]{4,2,3,1,0:T(8,128)(2,1)} %copy.196) | copy-start | bytes 26542084
  503.4 13.2 %copy-start.27 = (bf16[12,8,8,640]{3,2,1,0:T(8,128)(2,1)S(1)}, bf16[12,8,8,640]{3,2,1,0:T(8,128)(2,1)}, u32[]{:S(2)}) copy-start(bf16[12,8,8,640]{3,2,1,0:T(8,128)(2,1)} %neg.3) | copy-start | bytes 2949124
  532.3 0.7 copy-start.30
  532.3 1.3 copy-start.26
  532.3 490.3 %all-reduce.70.cloned.1.call-start = ((), (), s32[]{:S(2)}) async-start(), calls=%async_computation.6 | async-start | bytes 7372800 | tf_op jit(solution)/shard_map/psum | solution.py:155
  556.4 3.2 copy-start.6
  556.4 3.2 copy-start.25
  559.6 4.5 copy-start.29
  1022.6 3.0 copy-start.23
Sparse Core Ops, SparseCore 0:
  10.3 115.2 all-gather.4
  127.8 110.5 all-gather.2
  465.9 236.5 reduce-scatter.2
  706.4 237.0 reduce-scatter.4
  945.9 76.7 all-reduce.69
where the time goes:
time: 1040 us; the launch traced here: 1030 us
  waiting for transfers between devices  548 us (53%)
  matrix products  200 us (19%)
  local copies, waits for them, and re-layouts  181 us (17%)
  blocking collectives  50.6 us (5%)
  other arithmetic  37.2 us (4%)
  between operations  15.9 us (2%)
    reduce_scatter x1, waiting for transfers between devices, local(): lax.psum_scatter(totals[2].reshape(kernel_shape), 'wide', scatter_dimensi...  241 us
    reduce_scatter x1, waiting for transfers between devices, local(): lax.psum_scatter(totals[0].reshape(kernel_shape), 'wide', scatter_dimensi...  112 us
    dot_general x6, matrix products, conv_back(): lax.dot_general(gradient.reshape(-1, channels), kernel_mat, (((1,), (1,))...  107 us
    all_gather x1, waiting for transfers between devices, fetch_kernels(): lax.all_gather(kernel_one, 'wide', axis=2, tiled=True)  75.9 us
    unnamed x123, local copies, waits for them, and re-layouts  66.4 us
    psum x1, waiting for transfers between devices, local(): summed = lax.psum((shares[0], shares[1], shares[2], shares[3]), 'dp')  66.4 us
    squeeze x6, local copies, waits for them, and re-layouts, conv_back(): spread[:, :, :, 3 * row_off + col_off, :]  60.8 us
    dot_general x4, matrix products, kernel_partial(): lax.dot_general(tap_patches(activation), gradient.reshape(-1, channels),...  56.9 us
  transfers between devices with their start and end apart: 5, of which 5 were waited for; matrix products, arithmetic and copies ran while one was open for 18% of the time, Pallas kernels for 0%

commit v1 on v0

v1 whole, which is shorter than its diff:
```python
import functools

import jax
import jax.numpy as jnp
from jax import lax
from jax.experimental import pallas as pl
from jax.experimental.pallas import tpu as pltpu
from jax.sharding import PartitionSpec as P

F32 = jnp.float32
BF16 = jnp.bfloat16
MESH = pl.DeviceIdType.MESH


def leaky_relu(values):
    return jnp.where(values > 0, values, 0.2 * values)


def leak_slope(values):
    return jnp.where(values > 0, 1.0, 0.2).astype(F32)


def tap_patches(activation):
    batch_size, height, map_width, channels = activation.shape
    padded = jnp.pad(activation, ((0, 0), (1, 1), (1, 1), (0, 0)))
    tap_list = [
        padded[:, row_off : row_off + height, col_off : col_off + map_width, :]
        for row_off in range(3)
        for col_off in range(3)
    ]
    return jnp.stack(tap_list, axis=3).reshape(batch_size * height * map_width, 9 * channels)


def conv_apply(activation, kernel_mat, bias_row):
    result = jnp.dot(tap_patches(activation), kernel_mat, preferred_element_type=F32)
    return result.reshape(activation.shape[:3] + (kernel_mat.shape[1],)) + bias_row.astype(F32)


def conv_back(gradient, kernel_mat):
    batch_size, height, map_width, channels = gradient.shape
    in_channels = kernel_mat.shape[0] // 9
    spread = lax.dot_general(
        gradient.reshape(-1, channels), kernel_mat, (((1,), (1,)), ((), ())), preferred_element_type=F32
    )
    spread = spread.reshape(batch_size, height, map_width, 9, in_channels)
    summed = jnp.zeros((batch_size, height + 2, map_width + 2, in_channels), F32)
    for row_off in range(3):
        for col_off in range(3):
            summed = summed + jnp.pad(
                spread[:, :, :, 3 * row_off + col_off, :],
                ((0, 0), (row_off, 2 - row_off), (col_off, 2 - col_off), (0, 0)),
            )
    return summed[:, 1 : height + 1, 1 : map_width + 1, :]


def kernel_partial(activation, gradient):
    channels = gradient.shape[3]
    return lax.dot_general(
        tap_patches(activation),
        gradient.reshape(-1, channels),
        (((0,), (0,)), ((), ())),
        preferred_element_type=F32,
    )


def plain_local(real_images, replay_chains, langevin_noise, real_cot, chain_cot, kernel_one, bias_one, kernel_two, bias_two):
    def whole(kernel):
        gathered = lax.all_gather(kernel, "wide", axis=2, tiled=True)
        return gathered.reshape(9 * gathered.shape[2], gathered.shape[3])

    first, second = whole(kernel_one), whole(kernel_two)
    first_bias = lax.all_gather(bias_one, "wide", axis=0, tiled=True)
    second_bias = lax.all_gather(bias_two, "wide", axis=0, tiled=True)

    def hidden_of(values):
        lower = leaky_relu(values).astype(BF16)
        return lower, conv_apply(lower, first, first_bias)

    def x_grad(values, cot, hidden_grad):
        return cot.astype(F32) + leak_slope(values) * conv_back(hidden_grad, first)

    chain_inner = conv_back(chain_cot, second)
    state = replay_chains.astype(F32)
    for step_index in range(langevin_noise.shape[0]):
        _, hidden = hidden_of(state)
        hidden_grad = (chain_inner * leak_slope(hidden)).astype(BF16)
        state = state - x_grad(state, chain_cot, hidden_grad) + 0.01 * langevin_noise[step_index].astype(F32)
    real = real_images.astype(F32)
    real_lower, real_hidden = hidden_of(real)
    real_upper = leaky_relu(real_hidden).astype(BF16)
    block_output = real + conv_apply(real_upper, second, second_bias)
    sample_lower, sample_hidden = hidden_of(state)
    sample_upper = leaky_relu(sample_hidden).astype(BF16)
    real_hgrad = (conv_back(real_cot, second) * leak_slope(real_hidden)).astype(BF16)
    input_grad = x_grad(real, real_cot, real_hgrad)
    sample_hgrad = -((chain_inner * leak_slope(sample_hidden)).astype(BF16))

    def bias_sum(values):
        return jnp.sum(values.astype(F32), axis=(0, 1, 2))

    totals = (
        kernel_partial(real_lower, real_hgrad) + kernel_partial(sample_lower, sample_hgrad),
        bias_sum(real_hgrad) + bias_sum(sample_hgrad),
        kernel_partial(real_upper, real_cot) + kernel_partial(sample_upper, -chain_cot),
        bias_sum(real_cot) - bias_sum(chain_cot),
    )
    channels = kernel_one.shape[3]
    kernel_shape = (3, 3, channels, channels)
    shares = (
        lax.psum_scatter(totals[0].reshape(kernel_shape), "wide", scatter_dimension=2, tiled=True),
        lax.psum_scatter(totals[1], "wide", scatter_dimension=0, tiled=True),
        lax.psum_scatter(totals[2].reshape(kernel_shape), "wide", scatter_dimension=2, tiled=True),
        lax.psum_scatter(totals[3], "wide", scatter_dimension=0, tiled=True),
    )
    summed = lax.psum(shares, "dp")
    return (block_output, input_grad, state, summed[0], summed[1], summed[2], summed[3])


NW = 8
C = 640
CS = C // NW
PX = 768
RS = 9 * CS
GR = 3 * CS
LT = 128
TAPS = [(p - 1, q - 1) for p in range(3) for q in range(3)]

PB_CS = 2 * RS
PB_XS = PB_CS + 4 * 2 * GR
PB_YS = PB_XS + 4 * GR
PB_ZS = PB_YS + 2 * GR
PB_FS = PB_ZS + 2 * GR
OWN_ROW = 4 * GR

RIGHT, LEFT, YN, SIB, XN = range(5)


def tn(a, b):
    return lax.dot_general(a, b, (((0,), (0,)), ((), ())), preferred_element_type=F32)


def nt(a, b):
    return lax.dot_general(a, b, (((1,), (1,)), ((), ())), preferred_element_type=F32)


def nn(a, b):
    return jnp.dot(a, b, preferred_element_type=F32)


def leak(v):
    return jnp.where(v > 0, v, 0.2 * v)


def slope(v):
    return jnp.where(v > 0, 1.0, 0.2).astype(F32)


def inside(di, dj):
    lane = lax.broadcasted_iota(jnp.int32, (1, LT), 1)
    row, col = (lane // 8) % 8 + di, lane % 8 + dj
    return (row >= 0) & (row < 8) & (col >= 0) & (col < 8)


def turn(v, by):
    by %= LT
    return v if by == 0 else pltpu.roll(v, by, 1)


def moved(v, di, dj):
    if di == 0 and dj == 0:
        return v
    return jnp.where(inside(di, dj), turn(v, -(8 * di + dj)), jnp.zeros_like(v))


def al(row, by=16):
    return pl.multiple_of(row, by)


def body(
    xr, xc, nz, gr, gc, k1, k2, bt,
    o_blk, o_ig, o_fs, o_g1, o_g2, o_b,
    W, XIN, GT, NT, XRT, L, SI, H, HG, UP, PB, SP, G, OUT, BC, BT, BG,
    CR, XRV, YR, FXR, FCR,
    in_sem, own_sem, out_sem, b_ssem, b_rsem, g_ssem, g_rsem,
    cs_sem, cr_sem, xs_sem, xr_sem, ys_sem, yr_sem, zs_sem, zr_sem, fs_sem, fr_sem, f2s_sem, f2r_sem,
    bgs_sem, bgr_sem,
):
    dp, w = lax.axis_index("dp"), lax.axis_index("wide")
    x, c = lax.div(dp, 2), lax.rem(dp, 2)
    z, y = lax.div(w, 2), lax.rem(w, 2)
    d_sib = (x * 2 + 1 - c, w)
    d_x = ((1 - x) * 2 + c, w)
    d_y = (dp, z * 2 + 1 - y)
    d_right = (dp, w + 2)
    d_left = (dp, w - 2)
    own_g = c * (1 + x)
    oth_g = c * (2 - x)

    def ring_z(by):
        return lax.rem(z + by, 4)

    barrier = pltpu.get_barrier_semaphore()
    greeted = [d_sib, d_x] + [(dp, lax.rem(w + by, NW)) for by in range(1, NW)]
    for dev in greeted:
        pl.semaphore_signal(barrier, inc=1, device_id=dev, device_id_type=MESH)

    def own_copy(k):
        return pltpu.make_async_copy((k1, k2)[k], W.at[k * NW + w], own_sem.at[k])

    own_copy(0).start()
    own_copy(1).start()
    bt_copy = pltpu.make_async_copy(bt, BT.at[w], own_sem.at[2])
    bt_copy.start()
    sources = [xc, xr, gc, gr, nz.at[0], nz.at[1]]

    def in_copy(n):
        return pltpu.make_async_copy(sources[n], XIN.at[n % 2], in_sem.at[n % 2])

    in_copy(0).start()
    in_copy(1).start()
    own_copy(0).wait()
    own_copy(1).wait()
    bt_copy.wait()
    pl.semaphore_wait(barrier, len(greeted))

    devs = {RIGHT: d_right, LEFT: d_left, YN: d_y, SIB: d_sib, XN: d_x}

    def message(k, s, tap, way):
        part = W.at[k * NW + s, pl.ds(al(tap * CS), CS), :]
        return pltpu.make_async_remote_copy(
            src_ref=part, dst_ref=part, send_sem=g_ssem.at[way], recv_sem=g_rsem.at[k, s, tap],
            device_id=devs[way], device_id_type=MESH,
        )

    def arrive(k, s, tap):
        message(k, s, tap, YN).wait_recv()

    def events(k, m):
        def z_part(n, j):
            tap = own_g * 3 + j

            @pl.when(n == 0)
            def _():
                @pl.when(z < 3)
                def _():
                    message(k, w, tap, RIGHT).start()

                @pl.when(z > 0)
                def _():
                    message(k, w, tap, LEFT).start()

                message(k, w, tap, YN).start()

            def flow(zz, onward, may):
                s = zz * 2 + y
                arrive(k, s, tap)

                @pl.when(may)
                def _():
                    message(k, s, tap, onward).start()

                message(k, s, tap, YN).start()
                message(k, s, tap, SIB).start()

                @pl.when(c == 1)
                def _():
                    message(k, s, tap, XN).start()

            @pl.when((n >= 1) & (z - n >= 0))
            def _():
                flow(z - n, RIGHT, z < 3)

            @pl.when((n >= 1) & (z + n <= 3))
            def _():
                flow(z + n, LEFT, z > 0)

        def y_part(n, j):
            tap = own_g * 3 + j

            def flow(zz):
                s = zz * 2 + 1 - y
                arrive(k, s, tap)
                message(k, s, tap, SIB).start()

                @pl.when(c == 1)
                def _():
                    message(k, s, tap, XN).start()

            @pl.when(z - n >= 0)
            def _():
                flow(z - n)

            @pl.when((n >= 1) & (z + n <= 3))
            def _():
                flow(z + n)

        def x_part(n, j, yy, least):
            tap = oth_g * 3 + j

            def flow(zz):
                s = zz * 2 + yy
                arrive(k, s, tap)
                message(k, s, tap, SIB).start()

            @pl.when((c == 1) & (n >= least) & (z - n >= 0))
            def _():
                flow(z - n)

            @pl.when((c == 1) & (n >= 1) & (z + n <= 3))
            def _():
                flow(z + n)

        for lag, part in (
            (2, lambda n, j: x_part(n, j, 1 - y, 0)),
            (1, lambda n, j: x_part(n, j, y, 1)),
            (1, y_part),
            (0, z_part),
        ):
            at = m - lag

            @pl.when((at >= 0) & (at < 12))
            def _(part=part, at=at):
                at = jnp.maximum(at, 0)
                part(lax.div(at, 3), lax.rem(at, 3))

    def ready(k, s):
        @pl.when(s != w)
        def _():
            @pl.when(c == 0)
            def _():
                for tap in range(3, 9):
                    arrive(k, s, tap)

            @pl.when(c == 1)
            def _():
                for tap in range(3):
                    arrive(k, s, tap)

    def bias_message(by):
        return pltpu.make_async_remote_copy(
            src_ref=BT.at[w], dst_ref=BT.at[w], send_sem=b_ssem.at[by], recv_sem=b_rsem.at[w],
            device_id=(dp, lax.rem(w + by, NW)), device_id_type=MESH,
        )

    def bias_arrive(by):
        s = lax.rem(w + by, NW)
        pltpu.make_async_remote_copy(
            src_ref=BT.at[s], dst_ref=BT.at[s], send_sem=b_ssem.at[by], recv_sem=b_rsem.at[s],
            device_id=(dp, s), device_id_type=MESH,
        ).wait_recv()

    events(0, 0)
    for by in range(1, NW):
        bias_message(by).start()

    S0, I0 = 0, C

    for n in range(6):
        in_copy(n).wait()
        if n == 0:
            t = XIN[0].T.astype(F32)
            SI[S0 : S0 + C, :] = t
            L[0] = leak(t).astype(BF16)
        elif n == 1:
            t = XIN[1].T
            XRT[...] = t
            L[1] = leak(t.astype(F32)).astype(BF16)
        elif n < 4:
            GT[n - 2] = XIN[n % 2].T
        else:
            NT[n - 4] = XIN[n % 2].T
        if n + 2 < 6:
            in_copy(n + 2).start()
        events(0, n + 1) if n < 2 else None
    H[...] = jnp.zeros_like(H)
    events(0, 3)
    for by in range(1, NW):
        bias_arrive(by)

    def bias_columns(s, carry):
        for k in range(2):
            row = jnp.broadcast_to(BT[s, k : k + 1, :], (LT, LT))
            BC[k, pl.ds(al(s * CS), CS), :] = row.T[0:CS, :]
        return carry

    lax.fori_loop(0, NW, bias_columns, 0)

    def rows_of(s):
        return pl.ds(al(s * CS), CS)

    def cols(n):
        return slice(n * LT, (n + 1) * LT)

    def patches(load, row):
        for n in range(PX // LT):
            v = load(cols(n))
            for t, (di, dj) in enumerate(TAPS):
                PB[pl.ds(al(row + t * CS), CS), cols(n)] = moved(v, di, dj)

    def spread_back(k, s, cot, use):
        for n in range(PX // 256):
            SP[...] = nn(W[k * NW + s], cot[:, n * 256 : (n + 1) * 256])
            for h in range(2):
                total = None
                for t, (di, dj) in enumerate(TAPS):
                    v = moved(SP[t * CS : (t + 1) * CS, h * LT : (h + 1) * LT], -di, -dj)
                    total = v if total is None else total + v
                use(cols(2 * n + h), total)

    def take_first(s):
        ready(0, s)
        for part in range(2):
            patches(lambda at: L[part, rows_of(s), at], part * RS)
            H[part] += tn(W[s], PB[part * RS : (part + 1) * RS, :])

    def take_second(s):
        ready(1, s)

        def chain(at, inner):
            hid = H[0, rows_of(s), at] + BC[0, rows_of(s), :]
            SI[pl.ds(al(I0 + s * CS), CS), at] = inner
            HG[0, rows_of(s), at] = (inner * slope(hid)).astype(BF16)

        spread_back(1, s, GT.at[0], chain)

        def real(at, inner):
            hid = H[1, rows_of(s), at] + BC[0, rows_of(s), :]
            HG[1, rows_of(s), at] = (inner * slope(hid)).astype(BF16)
            UP[1, rows_of(s), at] = leak(hid).astype(BF16)

        spread_back(1, s, GT.at[1], real)

    def turns(q, take):
        @pl.when((q >= 0) & (q < 12))
        def _():
            n, part = lax.div(jnp.maximum(q, 0), 3), lax.rem(jnp.maximum(q, 0), 3)

            def one(u, carry):
                side, flip = lax.rem(u, 2), lax.div(u, 2)
                zz = z + (2 * side - 1) * n
                yy = y + flip - 2 * y * flip

                @pl.when((zz >= 0) & (zz <= 3) & ((n > 0) | (side == 0)))
                def _():
                    take(zz * 2 + yy)

                return carry

            lax.fori_loop(part, part + 1 + lax.div(part, 2), one, 0)

    def slot(r, carry):
        events(0, r)
        events(1, r - 12)
        turns(r - 5, take_first)
        turns(r - 17, take_second)
        return carry

    lax.fori_loop(4, 29, slot, 0)

    def whole_first():
        def build(s, carry):
            patches(lambda at: L[0, rows_of(s), at], s * RS)
            return carry

        lax.fori_loop(0, NW, build, 0)

        def product(n, carry):
            at = pl.ds(al(n * 256, 256), 256)
            H[0, :, at] = tn(W[0:NW].reshape(NW * RS, C), PB[:, at])
            return carry

        lax.fori_loop(0, PX // 256, product, 0)

    def whole_back():
        def build(s, carry):
            for n in range(PX // LT):
                v = HG[0, rows_of(s), cols(n)]
                for t, (di, dj) in enumerate(TAPS):
                    PB[pl.ds(al(t * C + s * CS), CS), cols(n)] = moved(v, -di, -dj)
            return carry

        lax.fori_loop(0, NW, build, 0)

        def product(n, carry):
            at = pl.ds(al(n * 256, 256), 256)
            left = jnp.concatenate(
                [
                    jnp.concatenate([W[s, t * CS : (t + 1) * CS, :] for s in range(NW)], axis=0)
                    for t in range(9)
                ],
                axis=1,
            )
            H[0, :, at] = nn(left, PB[:, at])
            return carry

        lax.fori_loop(0, PX // 256, product, 0)

    def step_state(k):
        def one(s, carry):
            for n in range(PX // LT):
                state = SI[pl.ds(al(S0 + s * CS), CS), cols(n)]
                pull = GT[0, rows_of(s), cols(n)].astype(F32) + slope(state) * H[0, rows_of(s), cols(n)]
                state = state - pull + 0.01 * NT[k, rows_of(s), cols(n)].astype(F32)
                SI[pl.ds(al(S0 + s * CS), CS), cols(n)] = state
                L[0, rows_of(s), cols(n)] = leak(state).astype(BF16)
            return carry

        lax.fori_loop(0, NW, one, 0)

    def hidden_grads(last):
        def one(s, carry):
            for n in range(PX // LT):
                hid = H[0, rows_of(s), cols(n)] + BC[0, rows_of(s), :]
                grad = (SI[pl.ds(al(I0 + s * CS), CS), cols(n)] * slope(hid)).astype(BF16)
                if last:
                    HG[0, rows_of(s), cols(n)] = -grad
                    UP[0, rows_of(s), cols(n)] = leak(hid).astype(BF16)
                    GT[0, rows_of(s), cols(n)] = -GT[0, rows_of(s), cols(n)]
                else:
                    HG[0, rows_of(s), cols(n)] = grad
            return carry

        lax.fori_loop(0, NW, one, 0)

    whole_back()
    step_state(0)
    whole_first()
    hidden_grads(False)
    whole_back()
    step_state(1)
    OUT[...] = SI[S0 : S0 + C, :].T

    def out_copy(ref, rows=PX):
        return pltpu.make_async_copy(OUT.at[0:rows], ref, out_sem)

    out_copy(o_fs).start()
    whole_first()
    hidden_grads(True)

    ones = jnp.ones((8, PX), BF16)
    BG[0, 0:8, :] = nt(ones, HG[0]) + nt(ones, HG[1])
    BG[0, 8:16, :] = nt(ones, GT[0]) + nt(ones, GT[1])

    def bg_send(src, dst, sem, dev):
        return pltpu.make_async_remote_copy(
            src_ref=BG.at[src], dst_ref=BG.at[dst], send_sem=bgs_sem.at[sem], recv_sem=bgr_sem.at[sem],
            device_id=dev, device_id_type=MESH,
        )

    def bg_step(i):
        @pl.when(i == 1)
        def _():
            bg_send(0, 3, 0, d_sib).start()

        @pl.when(i == 2)
        def _():
            bg_send(0, 3, 0, d_sib).wait()
            BG[1] = BG[0] + BG[3]
            bg_send(1, 4, 1, d_x).start()

        @pl.when(i == 4)
        def _():
            bg_send(1, 4, 1, d_x).wait()
            BG[2] = BG[1] + BG[4]
            bg_send(2, 5, 2, d_y).start()

        @pl.when(i == 6)
        def _():
            bg_send(2, 5, 2, d_y).wait()
            BG[6 + z] = BG[2] + BG[5]
            for by in range(1, 4):
                bg_send(6 + z, 6 + z, 2 + by, (dp, ring_z(by) * 2 + y)).start()

        @pl.when(i == 9)
        def _():
            for by in range(1, 4):
                bg_send(6 + z, 6 + z, 2 + by, (dp, ring_z(by) * 2 + y)).wait()
            BG[0] = BG[6] + BG[7] + BG[8] + BG[9]
            pltpu.make_async_copy(BG.at[0], o_b, own_sem.at[3]).start()

    def shard_of(a):
        p = lax.rem(a, 8)
        zz = ring_z(1 + lax.div(p, 2))
        yy = lax.rem(y + 1 + lax.rem(p, 2), 2)
        return zz, yy

    def first_block(s, buf):
        for part in range(2):
            patches(lambda at: L[part, rows_of(s), at], part * RS)
        G[buf] = nt(PB[0:RS, :], HG[0]) + nt(PB[RS : 2 * RS, :], HG[1])

        def keep(at, total):
            H[0, rows_of(s), at] = total

        spread_back(0, s, HG.at[1], keep)

    def second_block(s, buf, start):
        for part in range(2):
            patches(lambda at: UP[part, rows_of(s), at], part * RS)
        G[buf] = nt(PB[0:RS, :], GT[0]) + nt(PB[RS : 2 * RS, :], GT[1])
        add = tn(W[NW + s], PB[RS : 2 * RS, :])

        @pl.when(start)
        def _():
            H[1] = add

        @pl.when(jnp.logical_not(start))
        def _():
            H[1] += add

    def remote(src, dst, ss, rs, dev):
        return pltpu.make_async_remote_copy(
            src_ref=src, dst_ref=dst, send_sem=ss, recv_sem=rs, device_id=dev, device_id_type=MESH
        )

    def core_send(a, core):
        q = lax.rem(a, 4)
        rows = 2 * GR if core == 0 else GR
        return remote(
            PB.at[pl.ds(al(PB_CS + q * 2 * GR), rows), 0:C], CR.at[q, 0:rows], cs_sem.at[q], cr_sem.at[q], d_sib
        )

    def x_send(a):
        q = lax.rem(a, 4)
        return remote(PB.at[pl.ds(al(PB_XS + q * GR), GR), 0:C], XRV.at[q], xs_sem.at[q], xr_sem.at[q], d_x)

    def y_send(a, zz):
        q = lax.rem(lax.div(a, 2), 2)
        at = lax.div(a, 8) * 4 + zz
        return remote(PB.at[pl.ds(al(PB_YS + q * GR), GR), 0:C], YR.at[at], ys_sem.at[q], yr_sem.at[at], d_y)

    def z_send(a, by):
        q = lax.rem(lax.div(a, 2), 2)
        at = lax.div(a, 8) * 3 + by - 1
        land = XIN.at[lax.div(a, 8), pl.ds(al((by - 1) * GR), GR), :]
        return remote(
            PB.at[pl.ds(al(PB_ZS + q * GR), GR), 0:C], land, zs_sem.at[q], zr_sem.at[at], (dp, ring_z(by) * 2 + y)
        )

    def f_rows(turn_):
        return pl.ds(PB_FS + turn_ * GR, GR)

    def f_send(turn_):
        return remote(PB.at[f_rows(turn_), 0:C], FXR.at[turn_], fs_sem.at[turn_], fr_sem.at[turn_], d_x)

    def f2_own(turn_, core):
        to = FCR.at[turn_, 0:GR] if core == 0 else FCR.at[turn_, pl.ds(al((own_g - 1) * GR), GR)]
        return remote(PB.at[f_rows(turn_), 0:C], to, f2s_sem.at[turn_, 0], f2r_sem.at[turn_, 0], d_sib)

    def f2_oth(turn_):
        to = FCR.at[turn_, pl.ds(al((oth_g - 1) * GR), GR)]
        return remote(FXR.at[turn_], to, f2s_sem.at[turn_, 1], f2r_sem.at[turn_, 1], d_sib)

    def acc(a):
        return pl.ds(al(lax.rem(a, 4) * GR), GR)

    def reduce_step(i, carry):
        @pl.when(i < 16)
        def _():
            zz, yy = shard_of(i)
            s = zz * 2 + yy
            buf = lax.rem(i, 2)

            @pl.when(i < 8)
            def _():
                second_block(s, buf, i == 0)

            @pl.when(i >= 8)
            def _():
                first_block(s, buf)

            q = lax.rem(i, 4)
            base = PB_CS + q * 2 * GR

            @pl.when(c == 0)
            def _():
                @pl.when(i >= 4)
                def _():
                    core_send(i - 4, 0).wait_send()

                PB[pl.ds(al(base), 2 * GR), 0:C] = G[buf, GR : 3 * GR, :].astype(BF16)
                core_send(i, 0).start()

            @pl.when(c == 1)
            def _():
                @pl.when(i >= 4)
                def _():
                    core_send(i - 4, 1).wait_send()

                PB[pl.ds(al(base), GR), 0:C] = G[buf, 0:GR, :].astype(BF16)
                core_send(i, 1).start()

        @pl.when((i >= 1) & (i < 17))
        def _():
            a = i - 1
            q, buf = lax.rem(a, 4), lax.rem(a, 2)

            @pl.when(c == 0)
            def _():
                core_send(a, 1).wait_recv()
                SI[acc(a), 0:C] = G[buf, 0:GR, :] + CR[q, 0:GR, :].astype(F32)

            @pl.when(c == 1)
            def _():
                core_send(a, 0).wait_recv()

                @pl.when(a >= 4)
                def _():
                    x_send(a - 4).wait_send()

                PB[pl.ds(al(PB_XS + q * GR), GR), 0:C] = (
                    G[buf, pl.ds(al(oth_g * GR), GR), :]
                    + CR[q, pl.ds(al(jnp.maximum(oth_g - 1, 0) * GR), GR), :].astype(F32)
                ).astype(BF16)
                x_send(a).start()
                SI[acc(a), 0:C] = (
                    G[buf, pl.ds(al(own_g * GR), GR), :]
                    + CR[q, pl.ds(al(jnp.maximum(own_g - 1, 0) * GR), GR), :].astype(F32)
                )

        @pl.when((i >= 2) & (i < 18))
        def _():
            a = i - 2
            zz, yy = shard_of(a)

            @pl.when(c == 1)
            def _():
                x_send(a).wait_recv()
                SI[acc(a), 0:C] += XRV[lax.rem(a, 4)].astype(F32)

            @pl.when(lax.rem(a, 2) == 0)
            def _():
                @pl.when(a >= 4)
                def _():
                    y_send(a - 4, 0).wait_send()

                q = lax.rem(lax.div(a, 2), 2)
                PB[pl.ds(al(PB_YS + q * GR), GR), 0:C] = SI[acc(a), 0:C].astype(BF16)
                y_send(a, zz).start()

        @pl.when((i >= 5) & (i < 20) & (lax.rem(i, 2) == 1))
        def _():
            a = i - 4
            zz, yy = shard_of(a)
            y_send(a, zz).wait_recv()
            total = SI[acc(a), 0:C] + YR[lax.div(a, 8) * 4 + zz].astype(F32)
            pair = lax.div(lax.rem(a, 8), 2)
            q = lax.rem(lax.div(a, 2), 2)

            @pl.when(pair < 3)
            def _():
                @pl.when(a >= 5)
                def _():
                    z_send(a, 1).wait_send()

                PB[pl.ds(al(PB_ZS + q * GR), GR), 0:C] = total.astype(BF16)
                for by in range(1, 4):

                    @pl.when(pair == by - 1)
                    def _(by=by):
                        z_send(a, by).start()

            @pl.when(pair == 3)
            def _():
                SI[OWN_ROW : OWN_ROW + GR, 0:C] = total

        for turn_, ref in ((0, o_g2), (1, o_g1)):
            base = 8 * turn_

            @pl.when(i == base + 12)
            def _(turn_=turn_, base=base):
                total = SI[OWN_ROW : OWN_ROW + GR, 0:C]
                for by in range(1, 4):
                    z_send(base, by).wait_recv()
                    total = total + XIN[turn_, (by - 1) * GR : by * GR, :].astype(F32)
                PB[f_rows(turn_), 0:C] = total.astype(BF16)
                f_send(turn_).start()

            @pl.when(i == base + 14)
            def _(turn_=turn_):
                f_send(turn_).wait()

                @pl.when(c == 0)
                def _():
                    both = PB[f_rows(turn_), 0:C].astype(F32) + FXR[turn_].astype(F32)
                    PB[f_rows(turn_), 0:C] = both.astype(BF16)
                    f2_own(turn_, 0).start()

                @pl.when(c == 1)
                def _():
                    f2_own(turn_, 1).start()
                    f2_oth(turn_).start()

            @pl.when(i == base + 15)
            def _(turn_=turn_, ref=ref):
                out_copy(o_fs).wait()

                @pl.when(c == 0)
                def _():
                    f2_own(turn_, 0).wait_send()
                    for part in range(2):
                        got = FCR.at[turn_, part * GR : (part + 1) * GR]
                        remote(got, got, f2s_sem.at[turn_, part], f2r_sem.at[turn_, part], d_sib).wait_recv()
                    OUT[0:GR, :] = PB[f_rows(turn_), 0:C].astype(F32)
                    OUT[GR : 3 * GR, :] = FCR[turn_].astype(F32)

                @pl.when(c == 1)
                def _():
                    f2_own(turn_, 1).wait_send()
                    f2_oth(turn_).wait_send()
                    f2_own(turn_, 0).wait_recv()
                    OUT[0:GR, :] = FCR[turn_, 0:GR].astype(F32)
                    OUT[pl.ds(al(jnp.maximum(own_g, 1) * GR), GR), :] = PB[f_rows(turn_), 0:C].astype(F32)
                    OUT[pl.ds(al(jnp.maximum(oth_g, 1) * GR), GR), :] = FXR[turn_].astype(F32)

                out_copy(ref, RS).start()

        @pl.when(i == 8)
        def _():
            out_copy(o_fs).wait()
            for n in range(PX // LT):
                whole = XRT[:, cols(n)].astype(F32) + H[1, :, cols(n)] + BC[1]
                OUT[n * LT : (n + 1) * LT, :] = whole.T
            out_copy(o_blk).start()

        @pl.when(i == 16)
        def _():
            out_copy(o_g2, RS).wait()
            for n in range(PX // LT):
                whole = GT[1, :, cols(n)].astype(F32) + slope(XRT[:, cols(n)].astype(F32)) * H[0, :, cols(n)]
                OUT[n * LT : (n + 1) * LT, :] = whole.T
            out_copy(o_ig).start()

        bg_step(i)
        return carry

    lax.fori_loop(0, 24, reduce_step, 0)

    out_copy(o_g1, RS).wait()
    pltpu.make_async_copy(BG.at[0], o_b, own_sem.at[3]).wait()
    for by in range(1, NW):
        bias_message(by).wait_send()

    def drain(way, planes, rows):
        part = W.at[0:planes, 0:rows, :]
        remote(part, part, g_ssem.at[way], g_rsem.at[0, 0, 0], d_sib).wait_send()

    for zz in range(4):

        @pl.when(z == zz)
        def _(zz=zz):
            if zz < 3:
                drain(RIGHT, 2 * (zz + 1), GR)
            if zz > 0:
                drain(LEFT, 2 * (4 - zz), GR)

    drain(YN, 8, GR)

    @pl.when(c == 0)
    def _():
        drain(SIB, 14, GR)
        for a in range(12, 16):
            core_send(a, 0).wait_send()

    @pl.when(c == 1)
    def _():
        drain(SIB, 14, 2 * GR)
        drain(XN, 14, GR)
        for a in range(12, 16):
            core_send(a, 1).wait_send()
            x_send(a).wait_send()

    for a in (12, 14):
        y_send(a, 0).wait_send()
    z_send(11, 1).wait_send()
    z_send(13, 1).wait_send()


def kernel_local(real_images, replay_chains, langevin_noise, real_cot, chain_cot, kernel_one, bias_one, kernel_two, bias_two):
    def flat(values):
        return values.reshape(values.shape[:-4] + (PX, C))

    rows = jnp.stack([bias_one, bias_two]).astype(F32)
    bias_tile = jnp.pad(rows, ((0, 6), (0, LT - CS)))
    anywhere = pl.BlockSpec(memory_space=pl.ANY)
    dma = pltpu.SemaphoreType.DMA
    out_shape = [jax.ShapeDtypeStruct((PX, C), F32)] * 3 + [jax.ShapeDtypeStruct((RS, C), F32)] * 2
    out_shape += [jax.ShapeDtypeStruct((16, C), F32)]
    scratch = [
        pltpu.VMEM((2 * NW, RS, C), BF16),
        pltpu.VMEM((2, PX, C), BF16),
        pltpu.VMEM((2, C, PX), BF16),
        pltpu.VMEM((2, C, PX), BF16),
        pltpu.VMEM((C, PX), BF16),
        pltpu.VMEM((2, C, PX), BF16),
        pltpu.VMEM((2 * C, PX), F32),
        pltpu.VMEM((2, C, PX), F32),
        pltpu.VMEM((2, C, PX), BF16),
        pltpu.VMEM((2, C, PX), BF16),
        pltpu.VMEM((NW * RS, PX), BF16),
        pltpu.VMEM((RS, 256), F32),
        pltpu.VMEM((2, RS, C), F32),
        pltpu.VMEM((PX, C), F32),
        pltpu.VMEM((2, C, LT), F32),
        pltpu.VMEM((NW, 8, LT), F32),
        pltpu.VMEM((10, 16, C), F32),
        pltpu.VMEM((4, 2 * GR, C), BF16),
        pltpu.VMEM((4, GR, C), BF16),
        pltpu.VMEM((8, GR, C), BF16),
        pltpu.VMEM((2, GR, C), BF16),
        pltpu.VMEM((2, 2 * GR, C), BF16),
        dma((2,)), dma((4,)), dma, dma((NW,)), dma((NW,)), dma((5,)), dma((2, NW, 9)),
        dma((4,)), dma((4,)), dma((4,)), dma((4,)), dma((2,)), dma((8,)), dma((2,)), dma((6,)),
        dma((2,)), dma((2,)), dma((2, 2)), dma((2, 2)), dma((6,)), dma((6,)),
    ]
    blk, ig, fs, g1, g2, bsum = pl.pallas_call(
        body,
        out_shape=out_shape,
        in_specs=[anywhere] * 8,
        out_specs=[anywhere] * 6,
        scratch_shapes=scratch,
        compiler_params=pltpu.CompilerParams(
            collective_id=0, has_side_effects=True, vmem_limit_bytes=63 * 2**20
        ),
    )(
        flat(real_images), flat(replay_chains), flat(langevin_noise), flat(real_cot), flat(chain_cot),
        kernel_one.reshape(RS, C), kernel_two.reshape(RS, C), bias_tile,
    )
    at = lax.axis_index("wide") * CS
    shape = real_images.shape
    return (
        blk.reshape(shape), ig.reshape(shape), fs.reshape(shape),
        g1.reshape(kernel_one.shape), lax.dynamic_slice(bsum[0], (at,), (CS,)),
        g2.reshape(kernel_two.shape), lax.dynamic_slice(bsum[8], (at,), (CS,)),
    )


def solution(mesh):
    def local(real_images, *rest):
        kernel_one = rest[4]
        fits = (
            mesh.shape["dp"] == 4
            and mesh.shape["wide"] == NW
            and real_images.shape == (12, 8, 8, C)
            and kernel_one.shape == (3, 3, CS, C)
            and rest[1].shape[0] == 2
        )
        return (kernel_local if fits else plain_local)(real_images, *rest)

    return jax.shard_map(
        local,
        mesh=mesh,
        in_specs=(
            P(("dp", "wide"), None, None, None),
            P(("dp", "wide"), None, None, None),
            P(None, ("dp", "wide"), None, None, None),
            P(("dp", "wide"), None, None, None),
            P(("dp", "wide"), None, None, None),
            P(None, None, "wide", None),
            P("wide"),
            P(None, None, "wide", None),
            P("wide"),
        ),
        out_specs=(
            P(("dp", "wide"), None, None, None),
            P(("dp", "wide"), None, None, None),
            P(("dp", "wide"), None, None, None),
            P(None, None, "wide", None),
            P("wide"),
            P(None, None, "wide", None),
            P("wide"),
        ),
        check_vma=False,
    )
```

time: 1040 us -> 263 us (0.25)
  waiting for transfers between devices: 548 us -> 0 us
  Pallas kernels: 0 us -> 247 us
  matrix products: 200 us -> 0 us
  local copies, waits for them, and re-layouts: 181 us -> 12.3 us
  blocking collectives: 50.6 us -> 0 us
  other arithmetic: 37.2 us -> 1.27 us
  between operations: 15.9 us -> 0.65 us
    reduce_scatter x2 -> x0, waiting for transfers between devices: 353 us -> none  [the longest x1 241 us: local(): lax.psum_scatter(totals[2].reshape(kernel_shape), 'wide', scatter_dimensi...]
    pallas_call x0 -> x1, Pallas kernels: none -> 247 us  [kernel_local(): pl.pallas_call(body, out_shape=out_shape, in_specs=[anywhere] * 8, out_sp...]
    dot_general x13 -> x0, matrix products: 200 us -> none  [the longest x6 107 us: conv_back(): lax.dot_general(gradient.reshape(-1, channels), kernel_mat, (((1,), (1,))...]
    all_gather x2 -> x0, waiting for transfers between devices: 127 us -> none  [the longest x1 75.9 us: fetch_kernels(): lax.all_gather(kernel_one, 'wide', axis=2, tiled=True)]
    psum x1 -> x0, waiting for transfers between devices: 66.4 us -> none  [local(): summed = lax.psum((shares[0], shares[1], shares[2], shares[3]), 'dp')]
    squeeze x6 -> x0, local copies, waits for them, and re-layouts: 60.8 us -> none  [conv_back(): spread[:, :, :, 3 * row_off + col_off, :]]
    unnamed x123 -> x13, local copies, waits for them, and re-layouts: 66.4 us -> 11 us
    another operation x12 -> x0, local copies, waits for them, and re-layouts: 53.9 us -> none  [tap_patches(): jnp.stack(tap_list, axis=3)]
  transfers between devices with their start and end apart: 5 -> 0, of which waited for: 5 -> 0; matrix products, arithmetic and copies ran while one was open for 18% -> 0% of each run, Pallas kernels for 0% -> 0%
where the time goes in v1:
time: 263 us; the launch traced here: 261 us
  Pallas kernels  247 us (94%)
  local copies, waits for them, and re-layouts  12.3 us (5%)
    pallas_call x1, Pallas kernels, kernel_local(): pl.pallas_call(body, out_shape=out_shape, in_specs=[anywhere] * 8, out_sp...  247 us
    unnamed x13, local copies, waits for them, and re-layouts  11 us

profile of v1, /device:TPU:0, one launch (start us, length us, event | category | flops | bytes accessed | tf_op | source)
XLA Modules:
  0.0 261.1 jit_solution(8650458832453001425)
XLA Ops:
  0.6 1.3 fusion.6.bt
  1.9 246.9 %shard_map.144 = (f32[768,640]{1,0:T(8,128)}, f32[768,640]{1,0:T(8,128)}, f32[768,640]{1,0:T(8,128)}, f32[720,640]{1,0:T(8,128)}, f32[720,640]{1,0:T(8,128)}, /*index=5*/f32[16,640]{1,0:T(8,128)}) custom-call(bf16[768,640]{1,0:T(8,128)(2,1)} %bitcast.24, bf16[768,640]{1,0:T(8,128)(2,1)} %bitcast.25, bf16[2,768,640]{2,1,0:T(8,128)(2,1)} %bitcast.21, ...), custom_call_target="tpu_custom_call" | custom-call | tf_op jit(solution)/shard_map/pallas_call | solution.py:916
  248.8 0.8 fusion.7
  249.6 0.6 dynamic-slice_bitcast_fusion
  250.2 0.0 copy-start.1
  250.2 3.1 %copy.21 = f32[12,8,8,640]{3,2,1,0:T(8,128)} copy(f32[12,8,8,640]{3,2,1,0:T(8,128)} %bitcast.20) | data formatting | bytes 3932160
  253.3 0.0 copy-done.1
  253.3 0.0 copy-start
  253.3 1.3 copy.22
  254.6 1.0 copy-done
  255.5 0.0 copy-start.3
  255.5 1.3 copy.23
  256.8 0.9 copy-done.3
  257.7 0.0 copy-start.2
  257.7 1.2 copy.24
  259.0 0.9 copy-done.2
  259.9 1.2 copy.25
Async XLA Ops:
  250.2 3.1 %copy-start.1 = (f32[768,640]{1,0:T(8,128)S(1)}, f32[768,640]{1,0:T(8,128)}, u32[]{:S(2)}) copy-start(f32[768,640]{1,0:T(8,128)} %get-tuple-element.14) | copy-start | bytes 5898244
  253.3 2.3 copy-start
  255.5 2.2 copy-start.3
  257.7 2.2 copy-start.2

commit v2 on v1

--- a/solution.py
+++ b/solution.py
@@ -125,14 +125,14 @@
 LT = 128
 TAPS = [(p - 1, q - 1) for p in range(3) for q in range(3)]
 
-PB_CS = 2 * RS
-PB_XS = PB_CS + 4 * 2 * GR
-PB_YS = PB_XS + 4 * GR
-PB_ZS = PB_YS + 2 * GR
-PB_FS = PB_ZS + 2 * GR
-OWN_ROW = 4 * GR
+LAG_C, LAG_D = 2, 4
+XSLOTS = 2 * LAG_C
+F2 = 8 + LAG_D
+F3 = F2 + 1
 
 RIGHT, LEFT, YN, SIB, XN = range(5)
+LAG_Y, LAG_X = 3, 3
+LAG_T = max(LAG_X, LAG_Y + LAG_X - 1) + 3
 
 
 def tn(a, b):
@@ -177,10 +177,10 @@
 
 
 def body(
-    xr, xc, nz, gr, gc, k1, k2, bt,
+    xr, xc, nz, gr, gc, k1, k2, b1, b2,
     o_blk, o_ig, o_fs, o_g1, o_g2, o_b,
     W, XIN, GT, NT, XRT, L, SI, H, HG, UP, PB, SP, G, OUT, BC, BT, BG,
-    CR, XRV, YR, FXR, FCR,
+    CR, XRV, YR, FXR, FCR, CSB, YSB, ZSB, FSB,
     in_sem, own_sem, out_sem, b_ssem, b_rsem, g_ssem, g_rsem,
     cs_sem, cr_sem, xs_sem, xr_sem, ys_sem, yr_sem, zs_sem, zr_sem, fs_sem, fr_sem, f2s_sem, f2r_sem,
     bgs_sem, bgr_sem,
@@ -204,13 +204,17 @@
     for dev in greeted:
         pl.semaphore_signal(barrier, inc=1, device_id=dev, device_id_type=MESH)
 
+    def shard(k, s):
+        return pl.ds(al((k * NW + s) * RS), RS)
+
     def own_copy(k):
-        return pltpu.make_async_copy((k1, k2)[k], W.at[k * NW + w], own_sem.at[k])
+        return pltpu.make_async_copy((k1, k2)[k], W.at[shard(k, w)], own_sem.at[k])
 
     own_copy(0).start()
     own_copy(1).start()
-    bt_copy = pltpu.make_async_copy(bt, BT.at[w], own_sem.at[2])
-    bt_copy.start()
+    BT[w] = jnp.zeros((8, LT), F32)
+    BT[w, 0:1, 0:CS] = b1[...].astype(F32)
+    BT[w, 1:2, 0:CS] = b2[...].astype(F32)
     sources = [xc, xr, gc, gr, nz.at[0], nz.at[1]]
 
     def in_copy(n):
@@ -220,13 +224,12 @@
     in_copy(1).start()
     own_copy(0).wait()
     own_copy(1).wait()
-    bt_copy.wait()
     pl.semaphore_wait(barrier, len(greeted))
 
     devs = {RIGHT: d_right, LEFT: d_left, YN: d_y, SIB: d_sib, XN: d_x}
 
     def message(k, s, tap, way):
-        part = W.at[k * NW + s, pl.ds(al(tap * CS), CS), :]
+        part = W.at[pl.ds(al((k * NW + s) * RS + tap * CS), CS)]
         return pltpu.make_async_remote_copy(
             src_ref=part, dst_ref=part, send_sem=g_ssem.at[way], recv_sem=g_rsem.at[k, s, tap],
             device_id=devs[way], device_id_type=MESH,
@@ -311,9 +314,9 @@
                 flow(z + n)
 
         for lag, part in (
-            (2, lambda n, j: x_part(n, j, 1 - y, 0)),
-            (1, lambda n, j: x_part(n, j, y, 1)),
-            (1, y_part),
+            (LAG_Y + LAG_X, lambda n, j: x_part(n, j, 1 - y, 0)),
+            (LAG_X, lambda n, j: x_part(n, j, y, 1)),
+            (LAG_Y, y_part),
             (0, z_part),
         ):
             at = m - lag
@@ -395,11 +398,14 @@
         for n in range(PX // LT):
             v = load(cols(n))
             for t, (di, dj) in enumerate(TAPS):
-                PB[pl.ds(al(row + t * CS), CS), cols(n)] = moved(v, di, dj)
+                PB[n // 2, row + t * CS : row + (t + 1) * CS, cols(n % 2)] = moved(v, di, dj)
+
+    def held(row):
+        return jnp.concatenate([PB[m, row : row + RS, :] for m in range(PX // 256)], axis=1)
 
     def spread_back(k, s, cot, use):
         for n in range(PX // 256):
-            SP[...] = nn(W[k * NW + s], cot[:, n * 256 : (n + 1) * 256])
+            SP[...] = nn(W[shard(k, s)], cot[:, n * 256 : (n + 1) * 256])
             for h in range(2):
                 total = None
                 for t, (di, dj) in enumerate(TAPS):
@@ -411,15 +417,13 @@
         ready(0, s)
         for part in range(2):
             patches(lambda at: L[part, rows_of(s), at], part * RS)
-            H[part] += tn(W[s], PB[part * RS : (part + 1) * RS, :])
+            H[part] += tn(W[shard(0, s)], held(part * RS))
 
     def take_second(s):
         ready(1, s)
 
         def chain(at, inner):
-            hid = H[0, rows_of(s), at] + BC[0, rows_of(s), :]
             SI[pl.ds(al(I0 + s * CS), CS), at] = inner
-            HG[0, rows_of(s), at] = (inner * slope(hid)).astype(BF16)
 
         spread_back(1, s, GT.at[0], chain)
 
@@ -451,91 +455,98 @@
     def slot(r, carry):
         events(0, r)
         events(1, r - 12)
-        turns(r - 5, take_first)
-        turns(r - 17, take_second)
+        turns(r - LAG_T, take_first)
+        turns(r - 12 - LAG_T, take_second)
         return carry
 
-    lax.fori_loop(4, 29, slot, 0)
-
-    def whole_first():
-        def build(s, carry):
-            patches(lambda at: L[0, rows_of(s), at], s * RS)
-            return carry
-
-        lax.fori_loop(0, NW, build, 0)
-
-        def product(n, carry):
-            at = pl.ds(al(n * 256, 256), 256)
-            H[0, :, at] = tn(W[0:NW].reshape(NW * RS, C), PB[:, at])
-            return carry
-
-        lax.fori_loop(0, PX // 256, product, 0)
-
-    def whole_back():
-        def build(s, carry):
-            for n in range(PX // LT):
-                v = HG[0, rows_of(s), cols(n)]
+    lax.fori_loop(4, 24 + LAG_T, slot, 0)
+
+    def tile(n):
+        return slice(n * 256, (n + 1) * 256)
+
+    def half_tiles(n):
+        return [(h, cols(2 * n + h), cols(h)) for h in range(2)]
+
+    def shard_rows(s, base=0):
+        return slice(base + s * CS, base + (s + 1) * CS)
+
+    def step_state(k, n):
+        for s in range(NW):
+            rows = shard_rows(s)
+            for h, at, to in half_tiles(n):
+                state = SI[shard_rows(s, S0), at]
+                pull = GT[0, rows, at].astype(F32) + slope(state) * H[0, rows, at]
+                state = state - pull + 0.01 * NT[k, rows, at].astype(F32)
+                SI[shard_rows(s, S0), at] = state
+                low = leak(state).astype(BF16)
+                L[0, rows, at] = low
                 for t, (di, dj) in enumerate(TAPS):
-                    PB[pl.ds(al(t * C + s * CS), CS), cols(n)] = moved(v, -di, -dj)
-            return carry
-
-        lax.fori_loop(0, NW, build, 0)
-
-        def product(n, carry):
-            at = pl.ds(al(n * 256, 256), 256)
+                    PB[n, s * RS + t * CS : s * RS + (t + 1) * CS, to] = moved(low, di, dj)
+
+    def hidden_grad(n, sign, last, patch):
+        for s in range(NW):
+            rows = shard_rows(s)
+            for h, at, to in half_tiles(n):
+                hid = H[0, rows, at] + BC[0, rows, :]
+                grad = SI[shard_rows(s, I0), at] * slope(hid)
+                grad = (grad if sign is None else grad * sign).astype(BF16)
+                HG[0, rows, at] = grad
+                if last:
+                    UP[0, rows, at] = leak(hid).astype(BF16)
+                if patch:
+                    for t, (di, dj) in enumerate(TAPS):
+                        PB[n, t * C + s * CS : t * C + (s + 1) * CS, to] = moved(grad, -di, -dj)
+
+    def product_first(n):
+        total = None
+        for at in range(0, NW * RS, 2 * C):
+            rows = slice(at, min(at + 2 * C, NW * RS))
+            part = tn(W[rows, :], PB[n, rows, :])
+            total = part if total is None else total + part
+        H[0, :, tile(n)] = total
+
+    def product_back(n):
+        total = None
+        for t in range(0, 9, 2):
             left = jnp.concatenate(
                 [
-                    jnp.concatenate([W[s, t * CS : (t + 1) * CS, :] for s in range(NW)], axis=0)
-                    for t in range(9)
+                    jnp.concatenate([W[s * RS + u * CS : s * RS + (u + 1) * CS, :] for s in range(NW)], axis=0)
+                    for u in range(t, min(t + 2, 9))
                 ],
                 axis=1,
             )
-            H[0, :, at] = nn(left, PB[:, at])
-            return carry
-
-        lax.fori_loop(0, PX // 256, product, 0)
-
-    def step_state(k):
-        def one(s, carry):
-            for n in range(PX // LT):
-                state = SI[pl.ds(al(S0 + s * CS), CS), cols(n)]
-                pull = GT[0, rows_of(s), cols(n)].astype(F32) + slope(state) * H[0, rows_of(s), cols(n)]
-                state = state - pull + 0.01 * NT[k, rows_of(s), cols(n)].astype(F32)
-                SI[pl.ds(al(S0 + s * CS), CS), cols(n)] = state
-                L[0, rows_of(s), cols(n)] = leak(state).astype(BF16)
-            return carry
-
-        lax.fori_loop(0, NW, one, 0)
-
-    def hidden_grads(last):
-        def one(s, carry):
-            for n in range(PX // LT):
-                hid = H[0, rows_of(s), cols(n)] + BC[0, rows_of(s), :]
-                grad = (SI[pl.ds(al(I0 + s * CS), CS), cols(n)] * slope(hid)).astype(BF16)
-                if last:
-                    HG[0, rows_of(s), cols(n)] = -grad
-                    UP[0, rows_of(s), cols(n)] = leak(hid).astype(BF16)
-                    GT[0, rows_of(s), cols(n)] = -GT[0, rows_of(s), cols(n)]
-                else:
-                    HG[0, rows_of(s), cols(n)] = grad
-            return carry
-
-        lax.fori_loop(0, NW, one, 0)
-
-    whole_back()
-    step_state(0)
-    whole_first()
-    hidden_grads(False)
-    whole_back()
-    step_state(1)
+            part = nn(left, PB[n, t * C : min(t + 2, 9) * C, :])
+            total = part if total is None else total + part
+        H[0, :, tile(n)] = total
+
+    hidden_grad(0, None, False, True)
+
+    def langevin(k, carry):
+        hidden_grad(1, None, False, True)
+        product_back(0)
+        hidden_grad(2, None, False, True)
+        product_back(1)
+        step_state(k, 0)
+        product_back(2)
+        step_state(k, 1)
+        product_first(0)
+        step_state(k, 2)
+        product_first(1)
+        hidden_grad(0, (1 - 2 * k).astype(F32), True, True)
+        product_first(2)
+        return carry
+
+    lax.fori_loop(0, 2, langevin, 0)
+    hidden_grad(1, -1.0, True, False)
+    hidden_grad(2, -1.0, True, False)
+    for n in range(PX // LT):
+        GT[0, :, cols(n)] = -GT[0, :, cols(n)]
     OUT[...] = SI[S0 : S0 + C, :].T
 
     def out_copy(ref, rows=PX):
         return pltpu.make_async_copy(OUT.at[0:rows], ref, out_sem)
 
     out_copy(o_fs).start()
-    whole_first()
-    hidden_grads(True)
 
     ones = jnp.ones((8, PX), BF16)
     BG[0, 0:8, :] = nt(ones, HG[0]) + nt(ones, HG[1])
@@ -578,16 +589,22 @@
             BG[0] = BG[6] + BG[7] + BG[8] + BG[9]
             pltpu.make_async_copy(BG.at[0], o_b, own_sem.at[3]).start()
 
+    def places(pair):
+        return 2 - pair + 3 * lax.div(pair, 2) - 2 * lax.div(pair, 3)
+
     def shard_of(a):
         p = lax.rem(a, 8)
-        zz = ring_z(1 + lax.div(p, 2))
+        zz = ring_z(places(lax.div(p, 2)))
         yy = lax.rem(y + 1 + lax.rem(p, 2), 2)
         return zz, yy
+
+    def both_held():
+        return jnp.concatenate([held(0), held(RS)], axis=1)
 
     def first_block(s, buf):
         for part in range(2):
             patches(lambda at: L[part, rows_of(s), at], part * RS)
-        G[buf] = nt(PB[0:RS, :], HG[0]) + nt(PB[RS : 2 * RS, :], HG[1])
+        G[buf] = nt(both_held(), jnp.concatenate([HG[0], HG[1]], axis=1))
 
         def keep(at, total):
             H[0, rows_of(s), at] = total
@@ -597,8 +614,8 @@
     def second_block(s, buf, start):
         for part in range(2):
             patches(lambda at: UP[part, rows_of(s), at], part * RS)
-        G[buf] = nt(PB[0:RS, :], GT[0]) + nt(PB[RS : 2 * RS, :], GT[1])
-        add = tn(W[NW + s], PB[RS : 2 * RS, :])
+        G[buf] = nt(both_held(), jnp.concatenate([GT[0], GT[1]], axis=1))
+        add = tn(W[shard(1, s)], held(RS))
 
         @pl.when(start)
         def _():
@@ -614,52 +631,49 @@
         )
 
     def core_send(a, core):
-        q = lax.rem(a, 4)
+        q, h = lax.rem(a, 4), lax.rem(a, 2)
         rows = 2 * GR if core == 0 else GR
+        return remote(CSB.at[h, 0:rows], CR.at[q, 0:rows], cs_sem.at[h], cr_sem.at[q], d_sib)
+
+    def tap(j):
+        return slice(j * CS, (j + 1) * CS)
+
+    def x_out(h, j):
+        return lax.div(h, 2), pl.ds(al(lax.rem(h, 2) * GR + j * CS), CS), slice(0, C)
+
+    def x_send(a, j):
+        q, h = lax.rem(a, XSLOTS), lax.rem(a, 4)
+        return remote(NT.at[x_out(h, j)], XRV.at[q, tap(j)], xs_sem.at[h, j], xr_sem.at[q, j], d_x)
+
+    def y_send(a, zz, j):
+        q = lax.rem(lax.div(a, 2), 2)
+        return remote(YSB.at[q, tap(j)], YR.at[zz, tap(j)], ys_sem.at[q, j], yr_sem.at[zz, j], d_y)
+
+    def z_send(a, by, j):
+        q = lax.rem(lax.div(a, 2), 2)
+        land = XIN.at[lax.div(a, 8), pl.ds(al((by - 1) * GR + j * CS), CS), :]
         return remote(
-            PB.at[pl.ds(al(PB_CS + q * 2 * GR), rows), 0:C], CR.at[q, 0:rows], cs_sem.at[q], cr_sem.at[q], d_sib
+            ZSB.at[q, tap(j)], land, zs_sem.at[q, j], zr_sem.at[lax.div(a, 8), by - 1, j], (dp, ring_z(by) * 2 + y)
         )
 
-    def x_send(a):
-        q = lax.rem(a, 4)
-        return remote(PB.at[pl.ds(al(PB_XS + q * GR), GR), 0:C], XRV.at[q], xs_sem.at[q], xr_sem.at[q], d_x)
-
-    def y_send(a, zz):
-        q = lax.rem(lax.div(a, 2), 2)
-        at = lax.div(a, 8) * 4 + zz
-        return remote(PB.at[pl.ds(al(PB_YS + q * GR), GR), 0:C], YR.at[at], ys_sem.at[q], yr_sem.at[at], d_y)
-
-    def z_send(a, by):
-        q = lax.rem(lax.div(a, 2), 2)
-        at = lax.div(a, 8) * 3 + by - 1
-        land = XIN.at[lax.div(a, 8), pl.ds(al((by - 1) * GR), GR), :]
-        return remote(
-            PB.at[pl.ds(al(PB_ZS + q * GR), GR), 0:C], land, zs_sem.at[q], zr_sem.at[at], (dp, ring_z(by) * 2 + y)
-        )
-
-    def f_rows(turn_):
-        return pl.ds(PB_FS + turn_ * GR, GR)
-
-    def f_send(turn_):
-        return remote(PB.at[f_rows(turn_), 0:C], FXR.at[turn_], fs_sem.at[turn_], fr_sem.at[turn_], d_x)
-
-    def f2_own(turn_, core):
-        to = FCR.at[turn_, 0:GR] if core == 0 else FCR.at[turn_, pl.ds(al((own_g - 1) * GR), GR)]
-        return remote(PB.at[f_rows(turn_), 0:C], to, f2s_sem.at[turn_, 0], f2r_sem.at[turn_, 0], d_sib)
-
-    def f2_oth(turn_):
-        to = FCR.at[turn_, pl.ds(al((oth_g - 1) * GR), GR)]
-        return remote(FXR.at[turn_], to, f2s_sem.at[turn_, 1], f2r_sem.at[turn_, 1], d_sib)
-
-    def acc(a):
-        return pl.ds(al(lax.rem(a, 4) * GR), GR)
+    def f_send(turn_, j):
+        return remote(FSB.at[tap(j)], FXR.at[turn_, tap(j)], fs_sem.at[turn_, j], fr_sem.at[turn_, j], d_x)
+
+    def f2_send(turn_, src, row, j, n):
+        to = FCR.at[pl.ds(al(row + j * CS), CS)]
+        return remote(src.at[tap(j)], to, f2s_sem.at[turn_, n, j], f2r_sem.at[turn_, n, j], d_sib)
+
+    def acc(a, j):
+        half, odd = lax.div(a, 2), lax.rem(a, 2)
+        slot_ = lax.rem(half, 2) * (1 - odd) + (2 + lax.rem(half, 3)) * odd
+        return pl.ds(al(slot_ * GR + j * CS), CS)
 
     def reduce_step(i, carry):
         @pl.when(i < 16)
         def _():
             zz, yy = shard_of(i)
             s = zz * 2 + yy
-            buf = lax.rem(i, 2)
+            buf, h = lax.rem(i, 2), lax.rem(i, 2)
 
             @pl.when(i < 8)
             def _():
@@ -669,149 +683,151 @@
             def _():
                 first_block(s, buf)
 
-            q = lax.rem(i, 4)
-            base = PB_CS + q * 2 * GR
+            for core in range(2):
+
+                @pl.when(c == core)
+                def _(core=core):
+                    @pl.when(i >= 2)
+                    def _():
+                        core_send(i - 2, core).wait_send()
+
+                    if core == 0:
+                        CSB[h] = G[buf, GR : 3 * GR, :].astype(BF16)
+                    else:
+                        CSB[h, 0:GR] = G[buf, 0:GR, :].astype(BF16)
+                    core_send(i, core).start()
+
+        @pl.when((i >= 1) & (i < 17))
+        def _():
+            a = i - 1
+            q, h, buf = lax.rem(a, 4), lax.rem(a, 4), lax.rem(a, 2)
 
             @pl.when(c == 0)
             def _():
-                @pl.when(i >= 4)
-                def _():
-                    core_send(i - 4, 0).wait_send()
-
-                PB[pl.ds(al(base), 2 * GR), 0:C] = G[buf, GR : 3 * GR, :].astype(BF16)
-                core_send(i, 0).start()
+                core_send(a, 1).wait_recv()
+                for j in range(3):
+                    SI[acc(a, j), 0:C] = G[buf, tap(j), :] + CR[q, tap(j), :].astype(F32)
 
             @pl.when(c == 1)
             def _():
-                @pl.when(i >= 4)
-                def _():
-                    core_send(i - 4, 1).wait_send()
-
-                PB[pl.ds(al(base), GR), 0:C] = G[buf, 0:GR, :].astype(BF16)
-                core_send(i, 1).start()
-
-        @pl.when((i >= 1) & (i < 17))
-        def _():
-            a = i - 1
-            q, buf = lax.rem(a, 4), lax.rem(a, 2)
-
-            @pl.when(c == 0)
-            def _():
-                core_send(a, 1).wait_recv()
-                SI[acc(a), 0:C] = G[buf, 0:GR, :] + CR[q, 0:GR, :].astype(F32)
-
-            @pl.when(c == 1)
-            def _():
                 core_send(a, 0).wait_recv()
 
-                @pl.when(a >= 4)
-                def _():
-                    x_send(a - 4).wait_send()
-
-                PB[pl.ds(al(PB_XS + q * GR), GR), 0:C] = (
-                    G[buf, pl.ds(al(oth_g * GR), GR), :]
-                    + CR[q, pl.ds(al(jnp.maximum(oth_g - 1, 0) * GR), GR), :].astype(F32)
-                ).astype(BF16)
-                x_send(a).start()
-                SI[acc(a), 0:C] = (
-                    G[buf, pl.ds(al(own_g * GR), GR), :]
-                    + CR[q, pl.ds(al(jnp.maximum(own_g - 1, 0) * GR), GR), :].astype(F32)
-                )
-
-        @pl.when((i >= 2) & (i < 18))
-        def _():
-            a = i - 2
+                def theirs(g, j):
+                    return (
+                        G[buf, pl.ds(al(g * GR + j * CS), CS), :]
+                        + CR[q, pl.ds(al(jnp.maximum(g - 1, 0) * GR + j * CS), CS), :].astype(F32)
+                    )
+
+                for j in range(3):
+
+                    @pl.when(a >= 4)
+                    def _(j=j):
+                        x_send(a - 4, j).wait_send()
+
+                    NT[x_out(h, j)] = theirs(oth_g, j).astype(BF16)
+                    x_send(a, j).start()
+                for j in range(3):
+                    SI[acc(a, j), 0:C] = theirs(own_g, j)
+
+        @pl.when((i >= LAG_C) & (i < 16 + LAG_C))
+        def _():
+            a = i - LAG_C
             zz, yy = shard_of(a)
-
-            @pl.when(c == 1)
-            def _():
-                x_send(a).wait_recv()
-                SI[acc(a), 0:C] += XRV[lax.rem(a, 4)].astype(F32)
-
-            @pl.when(lax.rem(a, 2) == 0)
-            def _():
-                @pl.when(a >= 4)
-                def _():
-                    y_send(a - 4, 0).wait_send()
-
-                q = lax.rem(lax.div(a, 2), 2)
-                PB[pl.ds(al(PB_YS + q * GR), GR), 0:C] = SI[acc(a), 0:C].astype(BF16)
-                y_send(a, zz).start()
-
-        @pl.when((i >= 5) & (i < 20) & (lax.rem(i, 2) == 1))
-        def _():
-            a = i - 4
+            q = lax.rem(lax.div(a, 2), 2)
+            for j in range(3):
+
+                @pl.when(c == 1)
+                def _(j=j):
+                    x_send(a, j).wait_recv()
+                    SI[acc(a, j), 0:C] += XRV[lax.rem(a, XSLOTS), tap(j)].astype(F32)
+
+                @pl.when(lax.rem(a, 2) == 0)
+                def _(j=j):
+                    @pl.when(a >= 4)
+                    def _():
+                        y_send(a - 4, 0, j).wait_send()
+
+                    YSB[q, tap(j)] = SI[acc(a, j), 0:C].astype(BF16)
+                    y_send(a, zz, j).start()
+
+        @pl.when((i >= LAG_D + 1) & (i < 16 + LAG_D) & (lax.rem(i + LAG_D, 2) == 1))
+        def _():
+            a = i - LAG_D
             zz, yy = shard_of(a)
-            y_send(a, zz).wait_recv()
-            total = SI[acc(a), 0:C] + YR[lax.div(a, 8) * 4 + zz].astype(F32)
             pair = lax.div(lax.rem(a, 8), 2)
-            q = lax.rem(lax.div(a, 2), 2)
-
-            @pl.when(pair < 3)
-            def _():
-                @pl.when(a >= 5)
-                def _():
-                    z_send(a, 1).wait_send()
-
-                PB[pl.ds(al(PB_ZS + q * GR), GR), 0:C] = total.astype(BF16)
-                for by in range(1, 4):
-
-                    @pl.when(pair == by - 1)
-                    def _(by=by):
-                        z_send(a, by).start()
-
-            @pl.when(pair == 3)
-            def _():
-                SI[OWN_ROW : OWN_ROW + GR, 0:C] = total
+            q, turn_ = lax.rem(lax.div(a, 2), 2), lax.div(a, 8)
+            for j in range(3):
+                y_send(a, zz, j).wait_recv()
+                total = SI[acc(a, j), 0:C] + YR[zz, tap(j)].astype(F32)
+
+                @pl.when(pair < 3)
+                def _(j=j, total=total):
+                    @pl.when(a >= 5)
+                    def _():
+                        z_send(a, 1, j).wait_send()
+
+                    ZSB[q, tap(j)] = total.astype(BF16)
+                    for by in range(1, 4):
+
+                        @pl.when(places(pair) == by)
+                        def _(by=by):
+                            z_send(a, by, j).start()
+
+                @pl.when(pair == 3)
+                def _(j=j, total=total):
+                    whole = total
+                    for by in range(1, 4):
+                        z_send(a, by, j).wait_recv()
+                        at = slice((by - 1) * GR + j * CS, (by - 1) * GR + (j + 1) * CS)
+                        whole = whole + XIN[turn_, at, :].astype(F32)
+                    FSB[tap(j)] = whole.astype(BF16)
+                    f_send(turn_, j).start()
 
         for turn_, ref in ((0, o_g2), (1, o_g1)):
             base = 8 * turn_
 
-            @pl.when(i == base + 12)
-            def _(turn_=turn_, base=base):
-                total = SI[OWN_ROW : OWN_ROW + GR, 0:C]
-                for by in range(1, 4):
-                    z_send(base, by).wait_recv()
-                    total = total + XIN[turn_, (by - 1) * GR : by * GR, :].astype(F32)
-                PB[f_rows(turn_), 0:C] = total.astype(BF16)
-                f_send(turn_).start()
-
-            @pl.when(i == base + 14)
+            @pl.when(i == base + F2)
             def _(turn_=turn_):
-                f_send(turn_).wait()
+                for j in range(3):
+                    f_send(turn_, j).wait()
+
+                    @pl.when(c == 0)
+                    def _(j=j):
+                        both = FSB[tap(j)].astype(F32) + FXR[turn_, tap(j)].astype(F32)
+                        FSB[tap(j)] = both.astype(BF16)
+                        f2_send(turn_, FSB, 0, j, 0).start()
+
+                    @pl.when(c == 1)
+                    def _(j=j):
+                        f2_send(turn_, FSB, (own_g - 1) * GR, j, own_g - 1).start()
+                        f2_send(turn_, FXR.at[turn_], (oth_g - 1) * GR, j, oth_g - 1).start()
+
+            @pl.when(i == base + F3)
+            def _(turn_=turn_, ref=ref):
+                out_copy(o_fs).wait()
 
                 @pl.when(c == 0)
                 def _():
-                    both = PB[f_rows(turn_), 0:C].astype(F32) + FXR[turn_].astype(F32)
-                    PB[f_rows(turn_), 0:C] = both.astype(BF16)
-                    f2_own(turn_, 0).start()
+                    for j in range(3):
+                        OUT[tap(j), :] = FSB[tap(j)].astype(F32)
+                    for n in range(2):
+                        for j in range(3):
+                            f2_send(turn_, FSB, n * GR, j, n).wait_recv()
+                            at = slice(n * GR + j * CS, n * GR + (j + 1) * CS)
+                            OUT[GR + n * GR + j * CS : GR + n * GR + (j + 1) * CS, :] = FCR[at].astype(F32)
+                    for j in range(3):
+                        f2_send(turn_, FSB, 0, j, 0).wait_send()
 
                 @pl.when(c == 1)
                 def _():
-                    f2_own(turn_, 1).start()
-                    f2_oth(turn_).start()
-
-            @pl.when(i == base + 15)
-            def _(turn_=turn_, ref=ref):
-                out_copy(o_fs).wait()
-
-                @pl.when(c == 0)
-                def _():
-                    f2_own(turn_, 0).wait_send()
-                    for part in range(2):
-                        got = FCR.at[turn_, part * GR : (part + 1) * GR]
-                        remote(got, got, f2s_sem.at[turn_, part], f2r_sem.at[turn_, part], d_sib).wait_recv()
-                    OUT[0:GR, :] = PB[f_rows(turn_), 0:C].astype(F32)
-                    OUT[GR : 3 * GR, :] = FCR[turn_].astype(F32)
-
-                @pl.when(c == 1)
-                def _():
-                    f2_own(turn_, 1).wait_send()
-                    f2_oth(turn_).wait_send()
-                    f2_own(turn_, 0).wait_recv()
-                    OUT[0:GR, :] = FCR[turn_, 0:GR].astype(F32)
-                    OUT[pl.ds(al(jnp.maximum(own_g, 1) * GR), GR), :] = PB[f_rows(turn_), 0:C].astype(F32)
+                    OUT[pl.ds(al(jnp.maximum(own_g, 1) * GR), GR), :] = FSB[...].astype(F32)
                     OUT[pl.ds(al(jnp.maximum(oth_g, 1) * GR), GR), :] = FXR[turn_].astype(F32)
+                    for j in range(3):
+                        f2_send(turn_, FSB, 0, j, 0).wait_recv()
+                        OUT[tap(j), :] = FCR[tap(j)].astype(F32)
+                    for j in range(3):
+                        f2_send(turn_, FSB, 0, j, own_g - 1).wait_send()
+                        f2_send(turn_, FXR.at[turn_], 0, j, oth_g - 1).wait_send()
 
                 out_copy(ref, RS).start()
 
@@ -834,7 +850,7 @@
         bg_step(i)
         return carry
 
-    lax.fori_loop(0, 24, reduce_step, 0)
+    lax.fori_loop(0, 8 + F3 + 1, reduce_step, 0)
 
     out_copy(o_g1, RS).wait()
     pltpu.make_async_copy(BG.at[0], o_b, own_sem.at[3]).wait()
@@ -842,7 +858,7 @@
         bias_message(by).wait_send()
 
     def drain(way, planes, rows):
-        part = W.at[0:planes, 0:rows, :]
+        part = W.at[0 : planes * rows]
         remote(part, part, g_ssem.at[way], g_rsem.at[0, 0, 0], d_sib).wait_send()
 
     for zz in range(4):
@@ -859,35 +875,64 @@
     @pl.when(c == 0)
     def _():
         drain(SIB, 14, GR)
-        for a in range(12, 16):
+        for a in range(14, 16):
             core_send(a, 0).wait_send()
 
     @pl.when(c == 1)
     def _():
         drain(SIB, 14, 2 * GR)
         drain(XN, 14, GR)
+        for a in range(14, 16):
+            core_send(a, 1).wait_send()
         for a in range(12, 16):
-            core_send(a, 1).wait_send()
-            x_send(a).wait_send()
-
-    for a in (12, 14):
-        y_send(a, 0).wait_send()
-    z_send(11, 1).wait_send()
-    z_send(13, 1).wait_send()
+            for j in range(3):
+                x_send(a, j).wait_send()
+
+    for j in range(3):
+        for a in (12, 14):
+            y_send(a, 0, j).wait_send()
+        for a in (11, 13):
+            z_send(a, 1, j).wait_send()
+
+
+PIECES = 3
+
+
+def hand_over(blk, ig, fs, g1, g2, bsum, o_blk, o_ig, o_fs, o_g1, o_g2, o_b1, o_b2, wide, tall, sem):
+    loads, stores = [], []
+    for n, (src, dst) in enumerate(((blk, o_blk), (ig, o_ig), (fs, o_fs), (g1, o_g1), (g2, o_g2))):
+        rows = src.shape[0] // PIECES
+        for p in range(PIECES):
+            at = pl.ds(p * rows, rows)
+            held = wide.at[n, at] if n < 3 else tall.at[n - 3, at]
+            loads.append(pltpu.make_async_copy(src.at[at], held, sem.at[0, n, p]))
+            stores.append(pltpu.make_async_copy(held, dst.at[at], sem.at[1, n, p]))
+            loads[-1].start()
+    w = lax.axis_index("wide")
+    for s in range(NW):
+
+        @pl.when(w == s)
+        def _(s=s):
+            o_b1[...] = bsum[0:1, s * CS : (s + 1) * CS]
+            o_b2[...] = bsum[8:9, s * CS : (s + 1) * CS]
+
+    for load, store in zip(loads, stores):
+        load.wait()
+        store.start()
+    for store in stores:
+        store.wait()
 
 
 def kernel_local(real_images, replay_chains, langevin_noise, real_cot, chain_cot, kernel_one, bias_one, kernel_two, bias_two):
     def flat(values):
         return values.reshape(values.shape[:-4] + (PX, C))
 
-    rows = jnp.stack([bias_one, bias_two]).astype(F32)
-    bias_tile = jnp.pad(rows, ((0, 6), (0, LT - CS)))
     anywhere = pl.BlockSpec(memory_space=pl.ANY)
     dma = pltpu.SemaphoreType.DMA
     out_shape = [jax.ShapeDtypeStruct((PX, C), F32)] * 3 + [jax.ShapeDtypeStruct((RS, C), F32)] * 2
     out_shape += [jax.ShapeDtypeStruct((16, C), F32)]
     scratch = [
-        pltpu.VMEM((2 * NW, RS, C), BF16),
+        pltpu.VMEM((2 * NW * RS, C), BF16),
         pltpu.VMEM((2, PX, C), BF16),
         pltpu.VMEM((2, C, PX), BF16),
         pltpu.VMEM((2, C, PX), BF16),
@@ -897,7 +942,7 @@
         pltpu.VMEM((2, C, PX), F32),
         pltpu.VMEM((2, C, PX), BF16),
         pltpu.VMEM((2, C, PX), BF16),
-        pltpu.VMEM((NW * RS, PX), BF16),
+        pltpu.VMEM((PX // 256, NW * RS, 256), BF16),
         pltpu.VMEM((RS, 256), F32),
         pltpu.VMEM((2, RS, C), F32),
         pltpu.VMEM((PX, C), F32),
@@ -905,33 +950,43 @@
         pltpu.VMEM((NW, 8, LT), F32),
         pltpu.VMEM((10, 16, C), F32),
         pltpu.VMEM((4, 2 * GR, C), BF16),
+        pltpu.VMEM((XSLOTS, GR, C), BF16),
         pltpu.VMEM((4, GR, C), BF16),
-        pltpu.VMEM((8, GR, C), BF16),
         pltpu.VMEM((2, GR, C), BF16),
+        pltpu.VMEM((2 * GR, C), BF16),
         pltpu.VMEM((2, 2 * GR, C), BF16),
+        pltpu.VMEM((2, GR, C), BF16),
+        pltpu.VMEM((2, GR, C), BF16),
+        pltpu.VMEM((GR, C), BF16),
         dma((2,)), dma((4,)), dma, dma((NW,)), dma((NW,)), dma((5,)), dma((2, NW, 9)),
-        dma((4,)), dma((4,)), dma((4,)), dma((4,)), dma((2,)), dma((8,)), dma((2,)), dma((6,)),
-        dma((2,)), dma((2,)), dma((2, 2)), dma((2, 2)), dma((6,)), dma((6,)),
+        dma((2,)), dma((4,)), dma((4, 3)), dma((XSLOTS, 3)), dma((2, 3)), dma((4, 3)), dma((2, 3)), dma((2, 3, 3)),
+        dma((2, 3)), dma((2, 3)), dma((2, 2, 3)), dma((2, 2, 3)), dma((6,)), dma((6,)),
     ]
-    blk, ig, fs, g1, g2, bsum = pl.pallas_call(
+    made = pl.pallas_call(
         body,
         out_shape=out_shape,
-        in_specs=[anywhere] * 8,
+        in_specs=[anywhere] * 7 + [pl.BlockSpec(memory_space=pltpu.VMEM)] * 2,
         out_specs=[anywhere] * 6,
         scratch_shapes=scratch,
         compiler_params=pltpu.CompilerParams(
-            collective_id=0, has_side_effects=True, vmem_limit_bytes=63 * 2**20
+            collective_id=0, has_side_effects=True, vmem_limit_bytes=65400 * 2**10
         ),
     )(
         flat(real_images), flat(replay_chains), flat(langevin_noise), flat(real_cot), flat(chain_cot),
-        kernel_one.reshape(RS, C), kernel_two.reshape(RS, C), bias_tile,
+        kernel_one.reshape(RS, C), kernel_two.reshape(RS, C), bias_one.reshape(1, CS), bias_two.reshape(1, CS),
     )
-    at = lax.axis_index("wide") * CS
+    blk, ig, fs, g1, g2, first_bias, second_bias = pl.pallas_call(
+        hand_over,
+        out_shape=out_shape[:5] + [jax.ShapeDtypeStruct((1, CS), F32)] * 2,
+        in_specs=[anywhere] * 5 + [pl.BlockSpec(memory_space=pltpu.VMEM)],
+        out_specs=[anywhere] * 5 + [pl.BlockSpec(memory_space=pltpu.VMEM)] * 2,
+        scratch_shapes=[pltpu.VMEM((3, PX, C), F32), pltpu.VMEM((2, RS, C), F32), dma((2, 5, PIECES))],
+    )(*made)
     shape = real_images.shape
     return (
         blk.reshape(shape), ig.reshape(shape), fs.reshape(shape),
-        g1.reshape(kernel_one.shape), lax.dynamic_slice(bsum[0], (at,), (CS,)),
-        g2.reshape(kernel_two.shape), lax.dynamic_slice(bsum[8], (at,), (CS,)),
+        g1.reshape(kernel_one.shape), first_bias.reshape(CS),
+        g2.reshape(kernel_two.shape), second_bias.reshape(CS),
     )
 
 

time: 263 us -> 219 us (0.83)
  Pallas kernels: 247 us -> 218 us
  local copies, waits for them, and re-layouts: 12.3 us -> 0 us
    pallas_call x1 -> x2, Pallas kernels: 247 us -> 218 us  [the longest x1 209 us: kernel_local(): pl.pallas_call(body, out_shape=out_shape, in_specs=[anywhere] * 7 + [pl.B...]
    unnamed x13 -> x0, local copies, waits for them, and re-layouts: 11 us -> none
where the time goes in v2:
time: 219 us
  Pallas kernels  218 us (100%)
    pallas_call x1, Pallas kernels, kernel_local(): pl.pallas_call(body, out_shape=out_shape, in_specs=[anywhere] * 7 + [pl.B...  209 us
    pallas_call x1, Pallas kernels, kernel_local(): pl.pallas_call(hand_over, out_shape=out_shape[:5] + [jax.ShapeDtypeStruct...  8.79 us

profile of v2, /device:TPU:0, one launch (start us, length us, event | category | flops | bytes accessed | tf_op | source)
XLA Modules:
  0.0 219.1 jit_solution(12125619348148179297)
XLA Ops:
  0.6 209.5 %shard_map.144 = (f32[768,640]{1,0:T(8,128)}, f32[768,640]{1,0:T(8,128)}, f32[768,640]{1,0:T(8,128)}, f32[720,640]{1,0:T(8,128)}, f32[720,640]{1,0:T(8,128)}, /*index=5*/f32[16,640]{1,0:T(8,128)}) custom-call(bf16[768,640]{1,0:T(8,128)(2,1)} %bitcast.17, bf16[768,640]{1,0:T(8,128)(2,1)} %bitcast.18, bf16[2,768,640]{2,1,0:T(8,128)(2,1)} %bitcast.16, ...), custom_call_target="tpu_custom_call" | custom-call | tf_op jit(solution)/shard_map/pallas_call | solution.py:965
  210.1 8.8 %shard_map.145 = (f32[768,640]{1,0:T(8,128)}, f32[768,640]{1,0:T(8,128)}, f32[768,640]{1,0:T(8,128)}, f32[720,640]{1,0:T(8,128)}, f32[720,640]{1,0:T(8,128)}, /*index=5*/f32[1,80]{1,0:T(1,128)}, f32[1,80]{1,0:T(1,128)}) custom-call(f32[768,640]{1,0:T(8,128)} %get-tuple-element.20.blk, f32[768,640]{1,0:T(8,128)} %get-tuple-element.21.ig, ...), custom_call_target="tpu_custom_call" | custom-call | tf_op jit(solution)/shard_map/pallas_call | solution.py:978

commit v3 on v2

--- a/solution.py
+++ b/solution.py
@@ -125,13 +125,14 @@
 LT = 128
 TAPS = [(p - 1, q - 1) for p in range(3) for q in range(3)]
 
-LAG_C, LAG_D = 2, 4
-XSLOTS = 2 * LAG_C
+LAG_C, LAG_D = 3, 5
+XSLOTS = 2 * LAG_C - 2
 F2 = 8 + LAG_D
 F3 = F2 + 1
+FILL, TAIL = 1, 16
 
 RIGHT, LEFT, YN, SIB, XN = range(5)
-LAG_Y, LAG_X = 3, 3
+LAG_Y, LAG_X = 4, 4
 LAG_T = max(LAG_X, LAG_Y + LAG_X - 1) + 3
 
 
@@ -191,6 +192,9 @@
     d_sib = (x * 2 + 1 - c, w)
     d_x = ((1 - x) * 2 + c, w)
     d_y = (dp, z * 2 + 1 - y)
+    z_hi, z_lo = lax.div(z, 2), lax.rem(z, 2)
+    d_z1 = (dp, (2 * z_hi + 1 - z_lo) * 2 + y)
+    d_z2 = (dp, (2 * (1 - z_hi) + z_lo) * 2 + y)
     d_right = (dp, w + 2)
     d_left = (dp, w - 2)
     own_g = c * (1 + x)
@@ -548,9 +552,10 @@
 
     out_copy(o_fs).start()
 
-    ones = jnp.ones((8, PX), BF16)
-    BG[0, 0:8, :] = nt(ones, HG[0]) + nt(ones, HG[1])
-    BG[0, 8:16, :] = nt(ones, GT[0]) + nt(ones, GT[1])
+    def bias_terms():
+        ones = jnp.ones((8, PX), BF16)
+        BG[0, 0:8, :] = nt(ones, HG[0]) + nt(ones, HG[1])
+        BG[0, 8:16, :] = nt(ones, GT[0]) + nt(ones, GT[1])
 
     def bg_send(src, dst, sem, dev):
         return pltpu.make_async_remote_copy(
@@ -559,42 +564,41 @@
         )
 
     def bg_step(i):
-        @pl.when(i == 1)
-        def _():
+        @pl.when(i == 9)
+        def _():
+            bias_terms()
             bg_send(0, 3, 0, d_sib).start()
 
-        @pl.when(i == 2)
+        @pl.when(i == 10)
         def _():
             bg_send(0, 3, 0, d_sib).wait()
             BG[1] = BG[0] + BG[3]
             bg_send(1, 4, 1, d_x).start()
 
-        @pl.when(i == 4)
+        @pl.when(i == 12)
         def _():
             bg_send(1, 4, 1, d_x).wait()
             BG[2] = BG[1] + BG[4]
             bg_send(2, 5, 2, d_y).start()
 
-        @pl.when(i == 6)
+        @pl.when(i == 14)
         def _():
             bg_send(2, 5, 2, d_y).wait()
             BG[6 + z] = BG[2] + BG[5]
             for by in range(1, 4):
                 bg_send(6 + z, 6 + z, 2 + by, (dp, ring_z(by) * 2 + y)).start()
 
-        @pl.when(i == 9)
+        @pl.when(i == 17)
         def _():
             for by in range(1, 4):
                 bg_send(6 + z, 6 + z, 2 + by, (dp, ring_z(by) * 2 + y)).wait()
             BG[0] = BG[6] + BG[7] + BG[8] + BG[9]
             pltpu.make_async_copy(BG.at[0], o_b, own_sem.at[3]).start()
 
-    def places(pair):
-        return 2 - pair + 3 * lax.div(pair, 2) - 2 * lax.div(pair, 3)
-
     def shard_of(a):
         p = lax.rem(a, 8)
-        zz = ring_z(places(lax.div(p, 2)))
+        flips = 3 - lax.div(p, 2)
+        zz = 2 * lax.rem(z_hi + lax.div(flips, 2), 2) + lax.rem(z_lo + lax.rem(flips, 2), 2)
         yy = lax.rem(y + 1 + lax.rem(p, 2), 2)
         return zz, yy
 
@@ -606,24 +610,41 @@
             patches(lambda at: L[part, rows_of(s), at], part * RS)
         G[buf] = nt(both_held(), jnp.concatenate([HG[0], HG[1]], axis=1))
 
-        def keep(at, total):
-            H[0, rows_of(s), at] = total
-
-        spread_back(0, s, HG.at[1], keep)
-
-    def second_block(s, buf, start):
+    def second_block(s, buf):
         for part in range(2):
             patches(lambda at: UP[part, rows_of(s), at], part * RS)
         G[buf] = nt(both_held(), jnp.concatenate([GT[0], GT[1]], axis=1))
-        add = tn(W[shard(1, s)], held(RS))
-
-        @pl.when(start)
-        def _():
-            H[1] = add
-
-        @pl.when(jnp.logical_not(start))
-        def _():
-            H[1] += add
+
+    def real_piece(p, carry):
+        @pl.when(p < 8)
+        def _():
+            patches(lambda at: UP[1, rows_of(p), at], 2 * RS)
+            add = tn(W[shard(1, p)], held(2 * RS))
+
+            @pl.when(p == 0)
+            def _():
+                H[0] = add
+
+            @pl.when(p > 0)
+            def _():
+                H[0] += add
+
+        @pl.when(p >= 8)
+        def _():
+            s = p - 8
+
+            def keep(at, total):
+                H[1, rows_of(s), at] = total
+
+            spread_back(0, s, HG.at[1], keep)
+
+        return carry
+
+    def real_pieces(i):
+        def done(at):
+            return jnp.minimum(jnp.clip(at - FILL, 0, 8) + jnp.clip(at - TAIL, 0, 8) + 2 * jnp.clip(at - 20, 0, 4), 16)
+
+        lax.fori_loop(done(i), done(i + 1), real_piece, 0)
 
     def remote(src, dst, ss, rs, dev):
         return pltpu.make_async_remote_copy(
@@ -631,9 +652,9 @@
         )
 
     def core_send(a, core):
-        q, h = lax.rem(a, 4), lax.rem(a, 2)
+        h = lax.rem(a, 2)
         rows = 2 * GR if core == 0 else GR
-        return remote(CSB.at[h, 0:rows], CR.at[q, 0:rows], cs_sem.at[h], cr_sem.at[q], d_sib)
+        return remote(CSB.at[h, 0:rows], CR.at[h, 0:rows], cs_sem.at[h], cr_sem.at[h], d_sib)
 
     def tap(j):
         return slice(j * CS, (j + 1) * CS)
@@ -649,11 +670,11 @@
         q = lax.rem(lax.div(a, 2), 2)
         return remote(YSB.at[q, tap(j)], YR.at[zz, tap(j)], ys_sem.at[q, j], yr_sem.at[zz, j], d_y)
 
-    def z_send(a, by, j):
+    def z_send(a, pair, j):
         q = lax.rem(lax.div(a, 2), 2)
-        land = XIN.at[lax.div(a, 8), pl.ds(al((by - 1) * GR + j * CS), CS), :]
+        land = XIN.at[lax.div(a, 8), pair * GR + j * CS : pair * GR + (j + 1) * CS, :]
         return remote(
-            ZSB.at[q, tap(j)], land, zs_sem.at[q, j], zr_sem.at[lax.div(a, 8), by - 1, j], (dp, ring_z(by) * 2 + y)
+            ZSB.at[q, tap(j)], land, zs_sem.at[q, j], zr_sem.at[lax.div(a, 8), pair, j], d_z2 if pair == 1 else d_z1
         )
 
     def f_send(turn_, j):
@@ -669,19 +690,76 @@
         return pl.ds(al(slot_ * GR + j * CS), CS)
 
     def reduce_step(i, carry):
+        @pl.when((i >= LAG_C) & (i < 16 + LAG_C))
+        def _():
+            a = i - LAG_C
+            zz, yy = shard_of(a)
+            q = lax.rem(lax.div(a, 2), 2)
+            for j in range(3):
+
+                @pl.when(c == 1)
+                def _(j=j):
+                    x_send(a, j).wait_recv()
+                    SI[acc(a, j), 0:C] += XRV[lax.rem(a, XSLOTS), tap(j)].astype(F32)
+
+                @pl.when(lax.rem(a, 2) == 0)
+                def _(j=j):
+                    @pl.when(a >= 4)
+                    def _():
+                        y_send(a - 4, 0, j).wait_send()
+
+                    YSB[q, tap(j)] = SI[acc(a, j), 0:C].astype(BF16)
+                    y_send(a, zz, j).start()
+
         @pl.when(i < 16)
         def _():
             zz, yy = shard_of(i)
             s = zz * 2 + yy
+            buf = lax.rem(i, 2)
+
+            @pl.when(i < 8)
+            def _():
+                second_block(s, buf)
+
+            @pl.when(i >= 8)
+            def _():
+                first_block(s, buf)
+
+        @pl.when((i >= 1) & (i < 17))
+        def _():
+            a = i - 1
+            q, h, buf = lax.rem(a, 2), lax.rem(a, 4), lax.rem(a, 2)
+
+            @pl.when(c == 0)
+            def _():
+                core_send(a, 1).wait_recv()
+                for j in range(3):
+                    SI[acc(a, j), 0:C] = G[buf, tap(j), :] + CR[q, tap(j), :].astype(F32)
+
+            @pl.when(c == 1)
+            def _():
+                core_send(a, 0).wait_recv()
+
+                def theirs(g, j):
+                    return (
+                        G[buf, pl.ds(al(g * GR + j * CS), CS), :]
+                        + CR[q, pl.ds(al(jnp.maximum(g - 1, 0) * GR + j * CS), CS), :].astype(F32)
+                    )
+
+                for j in range(3):
+
+                    @pl.when(a >= 4)
+                    def _(j=j):
+                        x_send(a - 4, j).wait_send()
+
+                    NT[x_out(h, j)] = theirs(oth_g, j).astype(BF16)
+                    x_send(a, j).start()
+                for j in range(3):
+                    SI[acc(a, j), 0:C] = theirs(own_g, j)
+
+        @pl.when(i < 16)
+        def _():
             buf, h = lax.rem(i, 2), lax.rem(i, 2)
-
-            @pl.when(i < 8)
-            def _():
-                second_block(s, buf, i == 0)
-
-            @pl.when(i >= 8)
-            def _():
-                first_block(s, buf)
 
             for core in range(2):
 
@@ -696,59 +774,6 @@
                     else:
                         CSB[h, 0:GR] = G[buf, 0:GR, :].astype(BF16)
                     core_send(i, core).start()
-
-        @pl.when((i >= 1) & (i < 17))
-        def _():
-            a = i - 1
-            q, h, buf = lax.rem(a, 4), lax.rem(a, 4), lax.rem(a, 2)
-
-            @pl.when(c == 0)
-            def _():
-                core_send(a, 1).wait_recv()
-                for j in range(3):
-                    SI[acc(a, j), 0:C] = G[buf, tap(j), :] + CR[q, tap(j), :].astype(F32)
-
-            @pl.when(c == 1)
-            def _():
-                core_send(a, 0).wait_recv()
-
-                def theirs(g, j):
-                    return (
-                        G[buf, pl.ds(al(g * GR + j * CS), CS), :]
-                        + CR[q, pl.ds(al(jnp.maximum(g - 1, 0) * GR + j * CS), CS), :].astype(F32)
-                    )
-
-                for j in range(3):
-
-                    @pl.when(a >= 4)
-                    def _(j=j):
-                        x_send(a - 4, j).wait_send()
-
-                    NT[x_out(h, j)] = theirs(oth_g, j).astype(BF16)
-                    x_send(a, j).start()
-                for j in range(3):
-                    SI[acc(a, j), 0:C] = theirs(own_g, j)
-
-        @pl.when((i >= LAG_C) & (i < 16 + LAG_C))
-        def _():
-            a = i - LAG_C
-            zz, yy = shard_of(a)
-            q = lax.rem(lax.div(a, 2), 2)
-            for j in range(3):
-
-                @pl.when(c == 1)
-                def _(j=j):
-                    x_send(a, j).wait_recv()
-                    SI[acc(a, j), 0:C] += XRV[lax.rem(a, XSLOTS), tap(j)].astype(F32)
-
-                @pl.when(lax.rem(a, 2) == 0)
-                def _(j=j):
-                    @pl.when(a >= 4)
-                    def _():
-                        y_send(a - 4, 0, j).wait_send()
-
-                    YSB[q, tap(j)] = SI[acc(a, j), 0:C].astype(BF16)
-                    y_send(a, zz, j).start()
 
         @pl.when((i >= LAG_D + 1) & (i < 16 + LAG_D) & (lax.rem(i + LAG_D, 2) == 1))
         def _():
@@ -760,27 +785,28 @@
                 y_send(a, zz, j).wait_recv()
                 total = SI[acc(a, j), 0:C] + YR[zz, tap(j)].astype(F32)
 
+                def met(pair_, j=j):
+                    z_send(a, pair_, j).wait_recv()
+                    at = slice(pair_ * GR + j * CS, pair_ * GR + (j + 1) * CS)
+                    return XIN[turn_, at, :].astype(F32)
+
                 @pl.when(pair < 3)
-                def _(j=j, total=total):
+                def _(j=j):
                     @pl.when(a >= 5)
                     def _():
-                        z_send(a, 1, j).wait_send()
-
-                    ZSB[q, tap(j)] = total.astype(BF16)
-                    for by in range(1, 4):
-
-                        @pl.when(places(pair) == by)
-                        def _(by=by):
-                            z_send(a, by, j).start()
+                        z_send(a, 0, j).wait_send()
+
+                for pair_ in range(3):
+
+                    @pl.when(pair == pair_)
+                    def _(pair_=pair_, j=j, total=total, met=met):
+                        whole = total + met(0) if pair_ == 1 else total
+                        ZSB[q, tap(j)] = whole.astype(BF16)
+                        z_send(a, pair_, j).start()
 
                 @pl.when(pair == 3)
-                def _(j=j, total=total):
-                    whole = total
-                    for by in range(1, 4):
-                        z_send(a, by, j).wait_recv()
-                        at = slice((by - 1) * GR + j * CS, (by - 1) * GR + (j + 1) * CS)
-                        whole = whole + XIN[turn_, at, :].astype(F32)
-                    FSB[tap(j)] = whole.astype(BF16)
+                def _(j=j, total=total, met=met):
+                    FSB[tap(j)] = (total + met(1) + met(2)).astype(BF16)
                     f_send(turn_, j).start()
 
         for turn_, ref in ((0, o_g2), (1, o_g1)):
@@ -831,19 +857,21 @@
 
                 out_copy(ref, RS).start()
 
-        @pl.when(i == 8)
-        def _():
-            out_copy(o_fs).wait()
+        real_pieces(i)
+
+        @pl.when(i == F3 + 1)
+        def _():
+            out_copy(o_g2, RS).wait()
             for n in range(PX // LT):
-                whole = XRT[:, cols(n)].astype(F32) + H[1, :, cols(n)] + BC[1]
+                whole = XRT[:, cols(n)].astype(F32) + H[0, :, cols(n)] + BC[1]
                 OUT[n * LT : (n + 1) * LT, :] = whole.T
             out_copy(o_blk).start()
 
-        @pl.when(i == 16)
-        def _():
-            out_copy(o_g2, RS).wait()
+        @pl.when(i == 8 + F2)
+        def _():
+            out_copy(o_blk).wait()
             for n in range(PX // LT):
-                whole = GT[1, :, cols(n)].astype(F32) + slope(XRT[:, cols(n)].astype(F32)) * H[0, :, cols(n)]
+                whole = GT[1, :, cols(n)].astype(F32) + slope(XRT[:, cols(n)].astype(F32)) * H[1, :, cols(n)]
                 OUT[n * LT : (n + 1) * LT, :] = whole.T
             out_copy(o_ig).start()
 
@@ -892,7 +920,7 @@
         for a in (12, 14):
             y_send(a, 0, j).wait_send()
         for a in (11, 13):
-            z_send(a, 1, j).wait_send()
+            z_send(a, 0, j).wait_send()
 
 
 PIECES = 3
@@ -949,7 +977,7 @@
         pltpu.VMEM((2, C, LT), F32),
         pltpu.VMEM((NW, 8, LT), F32),
         pltpu.VMEM((10, 16, C), F32),
-        pltpu.VMEM((4, 2 * GR, C), BF16),
+        pltpu.VMEM((2, 2 * GR, C), BF16),
         pltpu.VMEM((XSLOTS, GR, C), BF16),
         pltpu.VMEM((4, GR, C), BF16),
         pltpu.VMEM((2, GR, C), BF16),
@@ -959,7 +987,7 @@
         pltpu.VMEM((2, GR, C), BF16),
         pltpu.VMEM((GR, C), BF16),
         dma((2,)), dma((4,)), dma, dma((NW,)), dma((NW,)), dma((5,)), dma((2, NW, 9)),
-        dma((2,)), dma((4,)), dma((4, 3)), dma((XSLOTS, 3)), dma((2, 3)), dma((4, 3)), dma((2, 3)), dma((2, 3, 3)),
+        dma((2,)), dma((2,)), dma((4, 3)), dma((XSLOTS, 3)), dma((2, 3)), dma((4, 3)), dma((2, 3)), dma((2, 3, 3)),
         dma((2, 3)), dma((2, 3)), dma((2, 2, 3)), dma((2, 2, 3)), dma((6,)), dma((6,)),
     ]
     made = pl.pallas_call(

time: 219 us -> 211 us (0.963)
  Pallas kernels: 218 us -> 210 us
    pallas_call x1, Pallas kernels: 209 us -> 201 us  [kernel_local(): pl.pallas_call(body, out_shape=out_shape, in_specs=[anywhere] * 7 + [pl.B...]
where the time goes in v3:
time: 211 us; the launch traced here: 210 us
  Pallas kernels  210 us (100%)
    pallas_call x1, Pallas kernels, kernel_local(): pl.pallas_call(body, out_shape=out_shape, in_specs=[anywhere] * 7 + [pl.B...  201 us
    pallas_call x1, Pallas kernels, kernel_local(): pl.pallas_call(hand_over, out_shape=out_shape[:5] + [jax.ShapeDtypeStruct...  8.79 us

profile of v3, /device:TPU:0, one launch (start us, length us, event | category | flops | bytes accessed | tf_op | source)
XLA Modules:
  0.0 210.4 jit_solution(15645264195751115446)
XLA Ops:
  0.6 200.8 %shard_map.144 = (f32[768,640]{1,0:T(8,128)}, f32[768,640]{1,0:T(8,128)}, f32[768,640]{1,0:T(8,128)}, f32[720,640]{1,0:T(8,128)}, f32[720,640]{1,0:T(8,128)}, /*index=5*/f32[16,640]{1,0:T(8,128)}) custom-call(bf16[768,640]{1,0:T(8,128)(2,1)} %bitcast.17, bf16[768,640]{1,0:T(8,128)(2,1)} %bitcast.18, bf16[2,768,640]{2,1,0:T(8,128)(2,1)} %bitcast.16, ...), custom_call_target="tpu_custom_call" | custom-call | tf_op jit(solution)/shard_map/pallas_call | solution.py:993
  201.5 8.8 %shard_map.145 = (f32[768,640]{1,0:T(8,128)}, f32[768,640]{1,0:T(8,128)}, f32[768,640]{1,0:T(8,128)}, f32[720,640]{1,0:T(8,128)}, f32[720,640]{1,0:T(8,128)}, /*index=5*/f32[1,80]{1,0:T(1,128)}, f32[1,80]{1,0:T(1,128)}) custom-call(f32[768,640]{1,0:T(8,128)} %get-tuple-element.20.blk, f32[768,640]{1,0:T(8,128)} %get-tuple-element.21.ig, ...), custom_call_target="tpu_custom_call" | custom-call | tf_op jit(solution)/shard_map/pallas_call | solution.py:1006

commit v4 on v3

--- a/solution.py
+++ b/solution.py
@@ -129,11 +129,10 @@
 XSLOTS = 2 * LAG_C - 2
 F2 = 8 + LAG_D
 F3 = F2 + 1
-FILL, TAIL = 1, 16
 
 RIGHT, LEFT, YN, SIB, XN = range(5)
 LAG_Y, LAG_X = 4, 4
-LAG_T = max(LAG_X, LAG_Y + LAG_X - 1) + 3
+LAG_T = LAG_Y + LAG_X
 
 
 def tn(a, b):
@@ -242,6 +241,9 @@
     def arrive(k, s, tap):
         message(k, s, tap, YN).wait_recv()
 
+    def by_z(k, j):
+        return (j == 2) & (k == 1)
+
     def events(k, m):
         def z_part(n, j):
             tap = own_g * 3 + j
@@ -266,7 +268,10 @@
                 def _():
                     message(k, s, tap, onward).start()
 
-                message(k, s, tap, YN).start()
+                @pl.when(jnp.logical_not(by_z(k, j)))
+                def _():
+                    message(k, s, tap, YN).start()
+
                 message(k, s, tap, SIB).start()
 
                 @pl.when(c == 1)
@@ -284,9 +289,18 @@
         def y_part(n, j):
             tap = own_g * 3 + j
 
-            def flow(zz):
+            def flow(zz, right, left):
                 s = zz * 2 + 1 - y
                 arrive(k, s, tap)
+
+                @pl.when(by_z(k, j) & right)
+                def _():
+                    message(k, s, tap, RIGHT).start()
+
+                @pl.when(by_z(k, j) & left)
+                def _():
+                    message(k, s, tap, LEFT).start()
+
                 message(k, s, tap, SIB).start()
 
                 @pl.when(c == 1)
@@ -295,11 +309,11 @@
 
             @pl.when(z - n >= 0)
             def _():
-                flow(z - n)
+                flow(z - n, z < 3, (n == 0) & (z > 0))
 
             @pl.when((n >= 1) & (z + n <= 3))
             def _():
-                flow(z + n)
+                flow(z + n, z < 0, z > 0)
 
         def x_part(n, j, yy, least):
             tap = oth_g * 3 + j
@@ -431,12 +445,9 @@
 
         spread_back(1, s, GT.at[0], chain)
 
-        def real(at, inner):
-            hid = H[1, rows_of(s), at] + BC[0, rows_of(s), :]
-            HG[1, rows_of(s), at] = (inner * slope(hid)).astype(BF16)
-            UP[1, rows_of(s), at] = leak(hid).astype(BF16)
-
-        spread_back(1, s, GT.at[1], real)
+        for n in range(PX // LT):
+            hid = H[1, rows_of(s), cols(n)] + BC[0, rows_of(s), :]
+            UP[1, rows_of(s), cols(n)] = leak(hid).astype(BF16)
 
     def turns(q, take):
         @pl.when((q >= 0) & (q < 12))
@@ -618,20 +629,29 @@
     def real_piece(p, carry):
         @pl.when(p < 8)
         def _():
-            patches(lambda at: UP[1, rows_of(p), at], 2 * RS)
-            add = tn(W[shard(1, p)], held(2 * RS))
-
-            @pl.when(p == 0)
+            def hidden_of(at, inner):
+                hid = H[1, rows_of(p), at] + BC[0, rows_of(p), :]
+                HG[1, rows_of(p), at] = (inner * slope(hid)).astype(BF16)
+
+            spread_back(1, p, GT.at[1], hidden_of)
+
+        @pl.when((p >= 8) & (p < 16))
+        def _():
+            s = p - 8
+            patches(lambda at: UP[1, rows_of(s), at], 2 * RS)
+            add = tn(W[shard(1, s)], held(2 * RS))
+
+            @pl.when(p == 8)
             def _():
                 H[0] = add
 
-            @pl.when(p > 0)
+            @pl.when(p > 8)
             def _():
                 H[0] += add
 
-        @pl.when(p >= 8)
-        def _():
-            s = p - 8
+        @pl.when(p >= 16)
+        def _():
+            s = p - 16
 
             def keep(at, total):
                 H[1, rows_of(s), at] = total
@@ -642,7 +662,7 @@
 
     def real_pieces(i):
         def done(at):
-            return jnp.minimum(jnp.clip(at - FILL, 0, 8) + jnp.clip(at - TAIL, 0, 8) + 2 * jnp.clip(at - 20, 0, 4), 16)
+            return jnp.minimum(jnp.clip(at, 0, 16) + jnp.clip(at - 16, 0, 8) + 2 * jnp.clip(at - 20, 0, 4), 24)
 
         lax.fori_loop(done(i), done(i + 1), real_piece, 0)
 
@@ -894,11 +914,11 @@
         @pl.when(z == zz)
         def _(zz=zz):
             if zz < 3:
-                drain(RIGHT, 2 * (zz + 1), GR)
+                drain(RIGHT, zz + 1, 7 * CS)
             if zz > 0:
-                drain(LEFT, 2 * (4 - zz), GR)
-
-    drain(YN, 8, GR)
+                drain(LEFT, 4 - zz, 7 * CS)
+
+    drain(YN, 21, CS)
 
     @pl.when(c == 0)
     def _():

time: 211 us -> 208 us (0.986)
  Pallas kernels: 210 us -> 206 us
    pallas_call x1, Pallas kernels: 201 us -> 197 us  [kernel_local(): pl.pallas_call(body, out_shape=out_shape, in_specs=[anywhere] * 7 + [pl.B...]
where the time goes in v4:
time: 208 us; the launch traced here: 207 us
  Pallas kernels  206 us (99%)
    pallas_call x1, Pallas kernels, kernel_local(): pl.pallas_call(body, out_shape=out_shape, in_specs=[anywhere] * 7 + [pl.B...  197 us
    pallas_call x1, Pallas kernels, kernel_local(): pl.pallas_call(hand_over, out_shape=out_shape[:5] + [jax.ShapeDtypeStruct...  8.79 us

profile of v4, /device:TPU:0, one launch (start us, length us, event | category | flops | bytes accessed | tf_op | source)
XLA Modules:
  0.0 206.8 jit_solution(2224536678697321306)
XLA Ops:
  0.6 197.2 %shard_map.144 = (f32[768,640]{1,0:T(8,128)}, f32[768,640]{1,0:T(8,128)}, f32[768,640]{1,0:T(8,128)}, f32[720,640]{1,0:T(8,128)}, f32[720,640]{1,0:T(8,128)}, /*index=5*/f32[16,640]{1,0:T(8,128)}) custom-call(bf16[768,640]{1,0:T(8,128)(2,1)} %bitcast.17, bf16[768,640]{1,0:T(8,128)(2,1)} %bitcast.18, bf16[2,768,640]{2,1,0:T(8,128)(2,1)} %bitcast.16, ...), custom_call_target="tpu_custom_call" | custom-call | tf_op jit(solution)/shard_map/pallas_call | solution.py:1013
  197.9 8.8 %shard_map.145 = (f32[768,640]{1,0:T(8,128)}, f32[768,640]{1,0:T(8,128)}, f32[768,640]{1,0:T(8,128)}, f32[720,640]{1,0:T(8,128)}, f32[720,640]{1,0:T(8,128)}, /*index=5*/f32[1,80]{1,0:T(1,128)}, f32[1,80]{1,0:T(1,128)}) custom-call(f32[768,640]{1,0:T(8,128)} %get-tuple-element.20.blk, f32[768,640]{1,0:T(8,128)} %get-tuple-element.21.ig, ...), custom_call_target="tpu_custom_call" | custom-call | tf_op jit(solution)/shard_map/pallas_call | solution.py:1026
